TPU v7x, 256 devices: a whole 4x4x8 slice. The times are simulated.
256 devices in a mesh: tm: 8 (over x_lo, y), wall: 4 (over x_hi, core), span: 8 (over z).
Axes of the slice: x: 4 (x_hi: 2, x_lo: 2; x = x_hi * 2 + x_lo), y: 4, z: 8, core: 2. Of those that a mesh axis runs over, the one named last changes fastest.
Arguments:
- starting_speed_vector: float32 [3, 8, 16, 128, 1024], P(None, 'tm', None, 'wall', 'span'), may hold values from -6 to 6
- driving_source: float32 [3, 8, 16, 128, 1024], P(None, 'tm', None, 'wall', 'span'), may hold values from -3 to 3
- viscosity: float32 [128], P('wall'), may hold values from 0.02 to 0.2
Outputs:
- orbit: float32 [3, 8, 16, 128, 1024], P(None, 'tm', None, 'wall', 'span')
- residual: float32 [3, 8, 16, 128, 1024], P(None, 'tm', None, 'wall', 'span')
All inputs are finite; a program needn't handle non-finite values.
Results may differ from a plain program's by a relative error of at most 0.0001.
Values sent between devices are 32-bit elements; how exact they have to be, the bound alone decides.
A program may use at most 64 MiB of HBM per device.

v0:
```python
import jax
import jax.numpy as jnp
from jax import lax
from jax.sharding import PartitionSpec as P

ITERS = 2


step_rate = 0.05


def with_halo(cells, sides, width, closed):
    for axis, dim in sides:
        count = lax.axis_size(axis)
        ends = count if closed else count - 1
        head = lax.slice_in_dim(cells, 0, width, axis=dim)
        tail = lax.slice_in_dim(cells, cells.shape[dim] - width, cells.shape[dim], axis=dim)
        cells = jnp.concatenate(
            [
                lax.ppermute(tail, axis, [(i, (i + 1) % count) for i in range(ends)]),
                cells,
                lax.ppermute(head, axis, [((i + 1) % count, i) for i in range(ends)]),
            ],
            axis=dim,
        )
    return cells


def partner_2(value, axis, bit):
    mask = 2**bit
    pairs = [(source, source ^ mask) for source in range(lax.axis_size(axis))]
    return lax.ppermute(value, axis, pairs)


def time_pair(values):
    padded_state = with_halo(values, (("tm", 1),), 1, True)
    return (padded_state[:, 2:], padded_state[:, :-2])


def wall_pair(values):
    padded_state = with_halo(values, (("wall", 3),), 1, False)
    return (padded_state[:, :, :, 2:], padded_state[:, :, :, :-2])


def span_pair(values):
    padded_state = with_halo(values, (("span", 4),), 1, True)
    return (padded_state[:, :, :, :, 2:], padded_state[:, :, :, :, :-2])


def along_flow(values):
    return (jnp.roll(values, -1, 2), jnp.roll(values, 1, 2))


def reflect(values):
    stack_size = values.shape[0]
    sign_row = jnp.where(jnp.arange(stack_size) % 3 == 1, -1.0, 1.0).astype(jnp.float32)
    sign_row = sign_row.reshape(stack_size, 1, 1, 1, 1)
    wall_bits = lax.axis_size("wall").bit_length() - 1
    time_bits = lax.axis_size("tm").bit_length() - 1
    partner = values
    for bit_index in list(range(wall_bits)) + [wall_bits + time_bits - 1]:
        partner = partner_2(partner, ("tm", "wall"), bit_index)
    partner = partner[:, :, :, ::-1, :]
    return partner * sign_row


def residual_of(present_state, mirrored, driving_source, viscous):
    ahead_time, behind_time = time_pair(present_state)
    neighbours = (along_flow(present_state), wall_pair(present_state), span_pair(present_state))
    slopes = [0.5 * (ahead - behind) for ahead, behind in neighbours]
    advect = (
        present_state[0:1] * slopes[0]
        + present_state[1:2] * slopes[1]
        + present_state[2:3] * slopes[2]
    )
    laplace = neighbours[0][0] + neighbours[0][1] - 2.0 * present_state
    laplace = laplace + (neighbours[1][0] + neighbours[1][1] - 2.0 * present_state)
    laplace = laplace + (neighbours[2][0] + neighbours[2][1] - 2.0 * present_state)
    residual_now = (
        0.5 * (ahead_time - behind_time)
        + advect
        - viscous * laplace
        + 0.5 * (present_state - mirrored)
        - driving_source
    )
    return (residual_now, neighbours, slopes)


def descent_part(neighbours, slopes, residual_now, viscous):
    ahead_time, behind_time = time_pair(residual_now)
    scaled = viscous * residual_now
    wall_ahead, wall_behind = wall_pair(jnp.concatenate((residual_now, scaled), 0))
    flow_ahead, flow_behind = along_flow(residual_now)
    span_ahead, span_behind = span_pair(residual_now)
    residual_pairs = (
        (flow_ahead, flow_behind),
        (wall_ahead[:3], wall_behind[:3]),
        (span_ahead, span_behind),
    )
    transport = jnp.stack(
        [jnp.sum(residual_now * slopes[component], axis=0) for component in range(3)]
    )
    second = None
    for axis_id in range(3):
        ahead_u = neighbours[axis_id][0][axis_id : axis_id + 1]
        behind_u = neighbours[axis_id][1][axis_id : axis_id + 1]
        term = 0.5 * (ahead_u * residual_pairs[axis_id][0] - behind_u * residual_pairs[axis_id][1])
        second = term if second is None else second + term
    diffused = viscous * flow_ahead + viscous * flow_behind - 2.0 * scaled
    diffused = diffused + (wall_ahead[3:] + wall_behind[3:] - 2.0 * scaled)
    diffused = diffused + (viscous * span_ahead + viscous * span_behind - 2.0 * scaled)
    return -0.5 * (ahead_time - behind_time) + transport - second - diffused


def local(starting_speed_vector, driving_source, viscosity):
    viscous = viscosity[None, None, None, :, None]
    present_state = starting_speed_vector
    residual_now = starting_speed_vector
    mirrored = starting_speed_vector
    for iteration in range(ITERS):
        mirrored = reflect(present_state)
        residual_now, neighbours, slopes = residual_of(
            present_state, mirrored, driving_source, viscous
        )
        local_part = descent_part(neighbours, slopes, residual_now, viscous)
        mirror_residual = reflect(residual_now)
        present_state = present_state - step_rate * (
            local_part + 0.5 * (residual_now - mirror_residual)
        )
    return (present_state, residual_now)


def solution(mesh):
    placed = (P(None, "tm", None, "wall", "span"), P(None, "tm", None, "wall", "span"), P("wall"))
    return jax.shard_map(
        local,
        mesh=mesh,
        in_specs=placed,
        out_specs=(P(None, "tm", None, "wall", "span"), P(None, "tm", None, "wall", "span")),
        check_vma=False,
    )
```

profile of v0, /device:TPU:1, one launch (start us, length us, event | category | flops | bytes accessed | tf_op | source)
XLA Modules:
  0.0 257.6 jit_solution(4203766372119515686)
XLA Ops:
  0.6 3.3 %collective-permute-start.6 = (f32[3,1,16,32,128]{4,3,2,1,0:T(8,128)}, f32[3,1,16,32,128]{4,3,2,1,0:T(8,128)S(1)}, u32[]{:S(2)}, u32[]{:S(2)}) collective-permute-start(f32[3,1,16,32,128]{4,3,2,1,0:T(8,128)} %param.3), channel_id=1, source_target_pairs={{0,8},{8,0},{16,24},{24,16},{32,40},{40,32},{48,56},{56,48},{64,72... | collective-permute-start | bytes 2359304 | tf_op jit(solution)/shard_map/ppermute | solution.py:32
  3.9 2.1 collective-permute-done.6
  6.0 1.0 collective-permute-start.7
  7.1 1.3 collective-permute-start.1
  8.4 2.3 collective-permute-start
  10.7 1.7 fusion.67
  12.7 1.7 collective-permute-start.5
  14.7 4.0 %collective-permute-start.4 = (f32[3,1,16,32,1]{3,2,4,1,0:T(8,128)S(1)}, f32[3,1,16,32,1]{3,2,4,1,0:T(8,128)S(1)}, u32[]{:S(2)}, u32[]{:S(2)}) collective-permute-start(f32[3,1,16,32,1]{3,2,4,1,0:T(8,128)S(1)} %copy.112), channel_id=1, source_target_pairs={{1,0},{2,1},{3,2},{4,3},{5,4},{6,5},{7,6},{0,7},{9,8},{10,9},{11,1... | collective-permute-start | bytes 18440 | tf_op jit(solution)/shard_map/ppermute | solution.py:22
  18.8 1.3 fusion.65
  20.1 6.3 %collective-permute-done.7 = f32[3,1,16,32,128]{4,3,2,1,0:T(8,128)} collective-permute-done((f32[3,1,16,32,128]{4,3,2,1,0:T(8,128)S(1)}, f32[3,1,16,32,128]{4,3,2,1,0:T(8,128)}, u32[]{:S(2)}, u32[]{:S(2)}) %collective-permute-start.7) | collective-permute-done | bytes 786464 | tf_op jit(solution)/shard_map/ppermute | solution.py:32
  26.4 4.0 %collective-permute-start.2 = (f32[3,1,16,1,128]{4,2,3,1,0:T(8,128)S(1)}, f32[3,1,16,1,128]{4,2,3,1,0:T(8,128)S(1)}, u32[]{:S(2)}, u32[]{:S(2)}) collective-permute-start(f32[3,1,16,1,128]{4,2,3,1,0:T(8,128)S(1)} %bitcast.76), channel_id=1, source_target_pairs={{8,0},{16,8},{24,16},{9,1},{17,9},{25,17},{10,2},{18,10},{26,18},{... | collective-permute-start | bytes 73736 | tf_op jit(solution)/shard_map/ppermute | solution.py:22
  30.4 4.0 %collective-permute-start.3 = (f32[3,1,16,1,128]{4,2,3,1,0:T(8,128)S(1)}, f32[3,1,16,1,128]{4,2,3,1,0:T(8,128)S(1)}, u32[]{:S(2)}, u32[]{:S(2)}) collective-permute-start(f32[3,1,16,1,128]{4,2,3,1,0:T(8,128)S(1)} %bitcast.74), channel_id=1, source_target_pairs={{0,8},{8,16},{16,24},{1,9},{9,17},{17,25},{2,10},{10,18},{18,26},{... | collective-permute-start | bytes 73736 | tf_op jit(solution)/shard_map/ppermute | solution.py:20
  35.7 25.0 %collective-permute-done.2 = f32[3,1,16,1,128]{4,2,3,1,0:T(8,128)S(1)} collective-permute-done((f32[3,1,16,1,128]{4,2,3,1,0:T(8,128)S(1)}, f32[3,1,16,1,128]{4,2,3,1,0:T(8,128)S(1)}, u32[]{:S(2)}, u32[]{:S(2)}) %collective-permute-start.2) | collective-permute-done | bytes 24608 | tf_op jit(solution)/shard_map/ppermute | solution.py:22
  60.8 1.4 fusion.54
  62.2 1.1 rev.12
  63.3 4.5 %multiply_reduce_fusion.4 = (f32[16,32,128]{2,1,0:T(8,128)}, f32[16,32,128]{2,1,0:T(8,128)}, f32[16,32,128]{2,1,0:T(8,128)}, f32[3,1,16,32,128]{4,3,2,1,0:T(8,128)S(1)}) fusion(f32[3,1,16,1,128]{4,3,2,1,0:T(1,128)S(1)} %bitcast.67, f32[3,1,16,32,128]{4,3,2,1,0:T(8,128)S(1)} %copy-done, f32[3,1,16,1,128]{4,3,2,1,0:T(1,128)S(1)} %bitcast.71, ...), kind=kLoop, calls=%fused_computation.90 | loop fusion | flops 9240576 | bytes 7925900 | tf_op jit(solution)/shard_map/reduce_sum | solution.py:101
  67.8 2.4 collective-permute-done.15
  70.3 0.8 collective-permute-start.16
  71.0 0.8 fusion.41
  71.9 3.6 %collective-permute-start.9 = (f32[3,1,16,32,128]{4,3,2,1,0:T(8,128)S(1)}, f32[3,1,16,32,128]{4,3,2,1,0:T(8,128)}, u32[]{:S(2)}, u32[]{:S(2)}) collective-permute-start(f32[3,1,16,32,128]{4,3,2,1,0:T(8,128)S(1)} %get-tuple-element.11), channel_id=1, source_target_pairs={{32,0},{64,32},{96,64},{128,96},{160,128},{192,160},{224,192},{0,2... | collective-permute-start | bytes 2359304 | tf_op jit(solution)/shard_map/ppermute | solution.py:22
  76.5 1.7 collective-permute-start.14
  78.2 4.2 %collective-permute-start.13 = (f32[3,1,16,32,1]{3,2,4,1,0:T(8,128)S(1)}, f32[3,1,16,32,1]{3,2,4,1,0:T(8,128)S(1)}, u32[]{:S(2)}, u32[]{:S(2)}) collective-permute-start(f32[3,1,16,32,1]{3,2,4,1,0:T(8,128)S(1)} %copy.90), channel_id=1, source_target_pairs={{1,0},{2,1},{3,2},{4,3},{5,4},{6,5},{7,6},{0,7},{9,8},{10,9},{11,1... | collective-permute-start | bytes 18440 | tf_op jit(solution)/shard_map/ppermute | solution.py:22
  82.4 8.7 %collective-permute-done.16 = f32[3,1,16,32,128]{4,3,2,1,0:T(8,128)} collective-permute-done((f32[3,1,16,32,128]{4,3,2,1,0:T(8,128)}, f32[3,1,16,32,128]{4,3,2,1,0:T(8,128)}, u32[]{:S(2)}, u32[]{:S(2)}) %collective-permute-start.16) | collective-permute-done | bytes 786464 | tf_op jit(solution)/shard_map/ppermute | solution.py:32
  91.2 1.3 fusion.62
  92.5 0.7 pad_maximum_fusion.31
  93.3 5.6 %collective-permute-start.12 = (f32[6,1,16,1,128]{4,2,3,1,0:T(8,128)}, f32[6,1,16,1,128]{4,2,3,1,0:T(8,128)S(1)}, u32[]{:S(2)}, u32[]{:S(2)}) collective-permute-start(f32[6,1,16,1,128]{4,2,3,1,0:T(8,128)} %bitcast.37), channel_id=1, source_target_pairs={{0,8},{8,16},{16,24},{1,9},{9,17},{17,25},{2,10},{10,18},{18,26},{... | collective-permute-start | bytes 147464 | tf_op jit(solution)/shard_map/ppermute | solution.py:20
  99.5 1.9 collective-permute-start.11
  101.4 2.0 copy.91
  103.4 2.0 copy.93
  105.4 17.2 %collective-permute-done.17 = f32[3,1,16,32,128]{4,3,2,1,0:T(8,128)S(1)} collective-permute-done((f32[3,1,16,32,128]{4,3,2,1,0:T(8,128)}, f32[3,1,16,32,128]{4,3,2,1,0:T(8,128)S(1)}, u32[]{:S(2)}, u32[]{:S(2)}) %collective-permute-start.17) | collective-permute-done | bytes 786464 | tf_op jit(solution)/shard_map/ppermute | solution.py:32
  122.5 1.1 rev.13
  123.6 2.0 collective-permute-done.11
  125.6 4.3 %fusion.28 = f32[3,1,16,32,128]{4,3,2,1,0:T(8,128)S(1)} fusion(f32[3,1,16,32,128]{4,3,2,1,0:T(8,128)S(1)} %copy-done, f32[6,1,16,1,128]{4,3,2,1,0:T(1,128)S(1)} %bitcast.72, f32[3,1,16,32,128]{4,3,2,1,0:T(8,128)S(1)} %broadcast_multiply_fusion.1, f32[3,1,16,32,128]{4,3,2,1,0:T(8,128)S(1)} %get-tuple-element.11, f32[6,1,16,1,128]{4,3,2,1,0:T(1,128)} %bitcast.11, ...), kind=kLoop, calls=%fused_computation.61 | loop fusion | flops 9437184 | bytes 9547916 | tf_op jit(solution)/shard_map/sub | solution.py:127
  130.0 2.3 collective-permute-done.24
  132.3 0.9 collective-permute-start.25
  133.2 3.6 %collective-permute-start.18 = (f32[3,1,16,32,128]{4,3,2,1,0:T(8,128)S(1)}, f32[3,1,16,32,128]{4,3,2,1,0:T(8,128)}, u32[]{:S(2)}, u32[]{:S(2)}) collective-permute-start(f32[3,1,16,32,128]{4,3,2,1,0:T(8,128)S(1)} %fusion.28), channel_id=1, source_target_pairs={{32,0},{64,32},{96,64},{128,96},{160,128},{192,160},{224,192},{0,2... | collective-permute-start | bytes 2359304 | tf_op jit(solution)/shard_map/ppermute | solution.py:22
  137.1 15.8 %collective-permute-done.25 = f32[3,1,16,32,128]{4,3,2,1,0:T(8,128)} collective-permute-done((f32[3,1,16,32,128]{4,3,2,1,0:T(8,128)S(1)}, f32[3,1,16,32,128]{4,3,2,1,0:T(8,128)}, u32[]{:S(2)}, u32[]{:S(2)}) %collective-permute-start.25) | collective-permute-done | bytes 786464 | tf_op jit(solution)/shard_map/ppermute | solution.py:32
  153.2 1.3 fusion.58
  155.2 1.7 collective-permute-start.23
  156.9 4.0 %collective-permute-start.22 = (f32[3,1,16,32,1]{3,2,4,1,0:T(8,128)S(1)}, f32[3,1,16,32,1]{3,2,4,1,0:T(8,128)S(1)}, u32[]{:S(2)}, u32[]{:S(2)}) collective-permute-start(f32[3,1,16,32,1]{3,2,4,1,0:T(8,128)S(1)} %copy.98), channel_id=1, source_target_pairs={{1,0},{2,1},{3,2},{4,3},{5,4},{6,5},{7,6},{0,7},{9,8},{10,9},{11,1... | collective-permute-start | bytes 18440 | tf_op jit(solution)/shard_map/ppermute | solution.py:22
  161.0 1.5 collective-permute-done.23
  162.5 4.7 %collective-permute-start.20 = (f32[3,1,16,1,128]{4,2,3,1,0:T(8,128)S(1)}, f32[3,1,16,1,128]{4,2,3,1,0:T(8,128)S(1)}, u32[]{:S(2)}, u32[]{:S(2)}) collective-permute-start(f32[3,1,16,1,128]{4,2,3,1,0:T(8,128)S(1)} %bitcast.77), channel_id=1, source_target_pairs={{8,0},{16,8},{24,16},{9,1},{17,9},{25,17},{10,2},{18,10},{26,18},{... | collective-permute-start | bytes 73736 | tf_op jit(solution)/shard_map/ppermute | solution.py:22
  167.2 2.8 %collective-permute-start.21 = (f32[3,1,16,1,128]{4,2,3,1,0:T(8,128)S(1)}, f32[3,1,16,1,128]{4,2,3,1,0:T(8,128)S(1)}, u32[]{:S(2)}, u32[]{:S(2)}) collective-permute-start(f32[3,1,16,1,128]{4,2,3,1,0:T(8,128)S(1)} %bitcast.75), channel_id=1, source_target_pairs={{0,8},{8,16},{16,24},{1,9},{9,17},{17,25},{2,10},{10,18},{18,26},{... | collective-permute-start | bytes 73736 | tf_op jit(solution)/shard_map/ppermute | solution.py:20
  170.8 16.2 %collective-permute-done.20 = f32[3,1,16,1,128]{4,2,3,1,0:T(8,128)S(1)} collective-permute-done((f32[3,1,16,1,128]{4,2,3,1,0:T(8,128)S(1)}, f32[3,1,16,1,128]{4,2,3,1,0:T(8,128)S(1)}, u32[]{:S(2)}, u32[]{:S(2)}) %collective-permute-start.20) | collective-permute-done | bytes 24608 | tf_op jit(solution)/shard_map/ppermute | solution.py:22
  187.0 1.4 fusion.47
  188.4 2.0 rev.14
  190.4 4.5 %multiply_reduce_fusion.1 = (f32[16,32,128]{2,1,0:T(8,128)}, f32[16,32,128]{2,1,0:T(8,128)}, f32[16,32,128]{2,1,0:T(8,128)}, f32[3,1,16,32,128]{4,3,2,1,0:T(8,128)S(1)}) fusion(f32[3,1,16,1,128]{4,3,2,1,0:T(1,128)S(1)} %bitcast.65, f32[3,1,16,32,128]{4,3,2,1,0:T(8,128)S(1)} %fusion.28, f32[3,1,16,1,128]{4,3,2,1,0:T(1,128)S(1)} %bitcast.69, ...), kind=kLoop, calls=%fused_computation.85 | loop fusion | flops 9240576 | bytes 7925900 | tf_op jit(solution)/shard_map/reduce_sum | solution.py:101
  194.9 2.4 collective-permute-done.33
  197.3 0.7 collective-permute-start.34
  197.9 0.7 fusion.39
  198.7 0.7 fusion.37
  199.4 3.6 %collective-permute-start.27 = (f32[3,1,16,32,128]{4,3,2,1,0:T(8,128)S(1)}, f32[3,1,16,32,128]{4,3,2,1,0:T(8,128)}, u32[]{:S(2)}, u32[]{:S(2)}) collective-permute-start(f32[3,1,16,32,128]{4,3,2,1,0:T(8,128)S(1)} %get-tuple-element.10), channel_id=1, source_target_pairs={{32,0},{64,32},{96,64},{128,96},{160,128},{192,160},{224,192},{0,2... | collective-permute-start | bytes 2359304 | tf_op jit(solution)/shard_map/ppermute | solution.py:22
  204.0 1.7 collective-permute-start.32
  205.7 4.0 %collective-permute-start.31 = (f32[3,1,16,32,1]{3,2,4,1,0:T(8,128)S(1)}, f32[3,1,16,32,1]{3,2,4,1,0:T(8,128)S(1)}, u32[]{:S(2)}, u32[]{:S(2)}) collective-permute-start(f32[3,1,16,32,1]{3,2,4,1,0:T(8,128)S(1)} %copy.106), channel_id=1, source_target_pairs={{1,0},{2,1},{3,2},{4,3},{5,4},{6,5},{7,6},{0,7},{9,8},{10,9},{11,1... | collective-permute-start | bytes 18440 | tf_op jit(solution)/shard_map/ppermute | solution.py:22
  209.7 8.4 %collective-permute-done.34 = f32[3,1,16,32,128]{4,3,2,1,0:T(8,128)} collective-permute-done((f32[3,1,16,32,128]{4,3,2,1,0:T(8,128)}, f32[3,1,16,32,128]{4,3,2,1,0:T(8,128)}, u32[]{:S(2)}, u32[]{:S(2)}) %collective-permute-start.34) | collective-permute-done | bytes 786464 | tf_op jit(solution)/shard_map/ppermute | solution.py:32
  218.8 1.3 fusion.55
  220.2 0.7 pad_maximum_fusion.29
  220.9 5.3 %collective-permute-start.30 = (f32[6,1,16,1,128]{4,2,3,1,0:T(8,128)}, f32[6,1,16,1,128]{4,2,3,1,0:T(8,128)S(1)}, u32[]{:S(2)}, u32[]{:S(2)}) collective-permute-start(f32[6,1,16,1,128]{4,2,3,1,0:T(8,128)} %bitcast.39), channel_id=1, source_target_pairs={{0,8},{8,16},{16,24},{1,9},{9,17},{17,25},{2,10},{10,18},{18,26},{... | collective-permute-start | bytes 147464 | tf_op jit(solution)/shard_map/ppermute | solution.py:20
  226.8 1.9 collective-permute-start.29
  228.8 1.1 copy.107
  229.9 2.0 copy.109
  231.9 18.1 %collective-permute-done.35 = f32[3,1,16,32,128]{4,3,2,1,0:T(8,128)} collective-permute-done((f32[3,1,16,32,128]{4,3,2,1,0:T(8,128)}, f32[3,1,16,32,128]{4,3,2,1,0:T(8,128)}, u32[]{:S(2)}, u32[]{:S(2)}) %collective-permute-start.35) | collective-permute-done | bytes 786464 | tf_op jit(solution)/shard_map/ppermute | solution.py:32
  250.0 1.9 rev.15
  252.6 4.9 %fusion.15 = f32[3,1,16,32,128]{4,3,2,1,0:T(8,128)} fusion(f32[3,1,16,32,128]{4,3,2,1,0:T(8,128)S(1)} %fusion.28, f32[6,1,16,1,128]{4,3,2,1,0:T(1,128)S(1)} %bitcast.73, f32[3,1,16,32,128]{4,3,2,1,0:T(8,128)S(1)} %broadcast_multiply_fusion, f32[3,1,16,32,128]{4,3,2,1,0:T(8,128)S(1)} %get-tuple-element.10, f32[6,1,16,1,128]{4,3,2,1,0:T(1,128)} %bitcast.29, ...), kind=kLoop, calls=%fused_computation.40 | loop fusion | flops 9437184 | bytes 9547916 | tf_op jit(solution)/shard_map/sub | solution.py:127
  (80 shorter events, 9.1 us)
Async XLA Ops:
  0.6 5.4 %collective-permute-start.6 = (f32[3,1,16,32,128]{4,3,2,1,0:T(8,128)}, f32[3,1,16,32,128]{4,3,2,1,0:T(8,128)S(1)}, u32[]{:S(2)}, u32[]{:S(2)}) collective-permute-start(f32[3,1,16,32,128]{4,3,2,1,0:T(8,128)} %param.3), channel_id=1, source_target_pairs={{0,8},{8,0},{16,24},{24,16},{32,40},{40,32},{48,56},{56,48},{64,72... | collective-permute-start | bytes 2359304 | tf_op jit(solution)/shard_map/ppermute | solution.py:32
  6.0 20.3 %collective-permute-start.7 = (f32[3,1,16,32,128]{4,3,2,1,0:T(8,128)S(1)}, f32[3,1,16,32,128]{4,3,2,1,0:T(8,128)}, u32[]{:S(2)}, u32[]{:S(2)}) collective-permute-start(f32[3,1,16,32,128]{4,3,2,1,0:T(8,128)S(1)} %collective-permute-done.6), channel_id=1, source_target_pairs={{0,16},{8,24},{16,0},{24,8},{32,48},{40,56},{48,32},{56,40},{64,80... | collective-permute-start | bytes 2359304 | tf_op jit(solution)/shard_map/ppermute | solution.py:32
  7.1 56.2 %collective-permute-start.1 = (f32[3,1,16,32,128]{4,3,2,1,0:T(8,128)}, f32[3,1,16,32,128]{4,3,2,1,0:T(8,128)}, u32[]{:S(2)}, u32[]{:S(2)}) collective-permute-start(f32[3,1,16,32,128]{4,3,2,1,0:T(8,128)} %param.3), channel_id=1, source_target_pairs={{0,32},{32,64},{64,96},{96,128},{128,160},{160,192},{192,224},{224... | collective-permute-start | bytes 2359304 | tf_op jit(solution)/shard_map/ppermute | solution.py:20
  8.4 54.9 %collective-permute-start = (f32[3,1,16,32,128]{4,3,2,1,0:T(8,128)}, f32[3,1,16,32,128]{4,3,2,1,0:T(8,128)}, u32[]{:S(2)}, u32[]{:S(2)}) collective-permute-start(f32[3,1,16,32,128]{4,3,2,1,0:T(8,128)} %param.3), channel_id=1, source_target_pairs={{32,0},{64,32},{96,64},{128,96},{160,128},{192,160},{224,192},{0,2... | collective-permute-start | bytes 2359304 | tf_op jit(solution)/shard_map/ppermute | solution.py:22
  12.3 6.4 %copy-start = (f32[3,1,16,32,128]{4,3,2,1,0:T(8,128)S(1)}, f32[3,1,16,32,128]{4,3,2,1,0:T(8,128)}, u32[]{:S(2)}) copy-start(f32[3,1,16,32,128]{4,3,2,1,0:T(8,128)} %param.3) | copy-start | bytes 2359300
  12.7 13.7 %collective-permute-start.5 = (f32[3,1,16,32,1]{3,2,4,1,0:T(8,128)S(1)}, f32[3,1,16,32,1]{3,2,4,1,0:T(8,128)S(1)}, u32[]{:S(2)}, u32[]{:S(2)}) collective-permute-start(f32[3,1,16,32,1]{3,2,4,1,0:T(8,128)S(1)} %copy.113), channel_id=1, source_target_pairs={{0,1},{1,2},{2,3},{3,4},{4,5},{5,6},{6,7},{7,0},{8,9},{9,10},{10,1... | collective-permute-start | bytes 18440 | tf_op jit(solution)/shard_map/ppermute | solution.py:20
  14.7 15.7 %collective-permute-start.4 = (f32[3,1,16,32,1]{3,2,4,1,0:T(8,128)S(1)}, f32[3,1,16,32,1]{3,2,4,1,0:T(8,128)S(1)}, u32[]{:S(2)}, u32[]{:S(2)}) collective-permute-start(f32[3,1,16,32,1]{3,2,4,1,0:T(8,128)S(1)} %copy.112), channel_id=1, source_target_pairs={{1,0},{2,1},{3,2},{4,3},{5,4},{6,5},{7,6},{0,7},{9,8},{10,9},{11,1... | collective-permute-start | bytes 18440 | tf_op jit(solution)/shard_map/ppermute | solution.py:22
  26.4 35.8 %collective-permute-start.8 = (f32[3,1,16,32,128]{4,3,2,1,0:T(8,128)}, f32[3,1,16,32,128]{4,3,2,1,0:T(8,128)S(1)}, u32[]{:S(2)}, u32[]{:S(2)}) collective-permute-start(f32[3,1,16,32,128]{4,3,2,1,0:T(8,128)} %collective-permute-done.7), channel_id=1, source_target_pairs={{0,128},{8,136},{16,144},{24,152},{32,160},{40,168},{48,176},{56,1... | collective-permute-start | bytes 2359304 | tf_op jit(solution)/shard_map/ppermute | solution.py:32
  26.4 34.3 %collective-permute-start.2 = (f32[3,1,16,1,128]{4,2,3,1,0:T(8,128)S(1)}, f32[3,1,16,1,128]{4,2,3,1,0:T(8,128)S(1)}, u32[]{:S(2)}, u32[]{:S(2)}) collective-permute-start(f32[3,1,16,1,128]{4,2,3,1,0:T(8,128)S(1)} %bitcast.76), channel_id=1, source_target_pairs={{8,0},{16,8},{24,16},{9,1},{17,9},{25,17},{10,2},{18,10},{26,18},{... | collective-permute-start | bytes 73736 | tf_op jit(solution)/shard_map/ppermute | solution.py:22
  30.4 30.4 %collective-permute-start.3 = (f32[3,1,16,1,128]{4,2,3,1,0:T(8,128)S(1)}, f32[3,1,16,1,128]{4,2,3,1,0:T(8,128)S(1)}, u32[]{:S(2)}, u32[]{:S(2)}) collective-permute-start(f32[3,1,16,1,128]{4,2,3,1,0:T(8,128)S(1)} %bitcast.74), channel_id=1, source_target_pairs={{0,8},{8,16},{16,24},{1,9},{9,17},{17,25},{2,10},{10,18},{18,26},{... | collective-permute-start | bytes 73736 | tf_op jit(solution)/shard_map/ppermute | solution.py:20
  63.3 7.7 %copy-start.4 = (f32[3,1,15,32,128]{4,3,2,1,0:T(8,128)S(1)}, f32[3,1,15,32,128]{4,3,2,1,0:T(8,128)}, u32[]{:S(2)}) copy-start(f32[3,1,15,32,128]{4,3,2,1,0:T(8,128)} %get-tuple-element.50) | copy-start | bytes 2211844
  63.3 7.7 %copy-start.5 = (f32[3,1,15,32,128]{4,3,2,1,0:T(8,128)S(1)}, f32[3,1,15,32,128]{4,3,2,1,0:T(8,128)}, u32[]{:S(2)}) copy-start(f32[3,1,15,32,128]{4,3,2,1,0:T(8,128)} %get-tuple-element.51) | copy-start | bytes 2211844
  67.8 2.4 collective-permute-start.15
  70.3 20.8 %collective-permute-start.16 = (f32[3,1,16,32,128]{4,3,2,1,0:T(8,128)}, f32[3,1,16,32,128]{4,3,2,1,0:T(8,128)}, u32[]{:S(2)}, u32[]{:S(2)}) collective-permute-start(f32[3,1,16,32,128]{4,3,2,1,0:T(8,128)} %collective-permute-done.15), channel_id=1, source_target_pairs={{0,16},{8,24},{16,0},{24,8},{32,48},{40,56},{48,32},{56,40},{64,80... | collective-permute-start | bytes 2359304 | tf_op jit(solution)/shard_map/ppermute | solution.py:32
  71.9 53.7 %collective-permute-start.10 = (f32[3,1,16,32,128]{4,3,2,1,0:T(8,128)S(1)}, f32[3,1,16,32,128]{4,3,2,1,0:T(8,128)}, u32[]{:S(2)}, u32[]{:S(2)}) collective-permute-start(f32[3,1,16,32,128]{4,3,2,1,0:T(8,128)S(1)} %get-tuple-element.11), channel_id=1, source_target_pairs={{0,32},{32,64},{64,96},{96,128},{128,160},{160,192},{192,224},{224... | collective-permute-start | bytes 2359304 | tf_op jit(solution)/shard_map/ppermute | solution.py:20
  71.9 53.7 %collective-permute-start.9 = (f32[3,1,16,32,128]{4,3,2,1,0:T(8,128)S(1)}, f32[3,1,16,32,128]{4,3,2,1,0:T(8,128)}, u32[]{:S(2)}, u32[]{:S(2)}) collective-permute-start(f32[3,1,16,32,128]{4,3,2,1,0:T(8,128)S(1)} %get-tuple-element.11), channel_id=1, source_target_pairs={{32,0},{64,32},{96,64},{128,96},{160,128},{192,160},{224,192},{0,2... | collective-permute-start | bytes 2359304 | tf_op jit(solution)/shard_map/ppermute | solution.py:22
  75.7 15.3 %copy-start.10 = (f32[32]{0:T(128)S(1)}, f32[32]{0:T(128)}, u32[]{:S(2)}) copy-start(f32[32]{0:T(128)} %param.5) | copy-start | bytes 388
  76.5 16.8 %collective-permute-start.14 = (f32[3,1,16,32,1]{3,2,4,1,0:T(8,128)S(1)}, f32[3,1,16,32,1]{3,2,4,1,0:T(8,128)S(1)}, u32[]{:S(2)}, u32[]{:S(2)}) collective-permute-start(f32[3,1,16,32,1]{3,2,4,1,0:T(8,128)S(1)} %copy.92), channel_id=1, source_target_pairs={{0,1},{1,2},{2,3},{3,4},{4,5},{5,6},{6,7},{7,0},{8,9},{9,10},{10,1... | collective-permute-start | bytes 18440 | tf_op jit(solution)/shard_map/ppermute | solution.py:20
  78.2 20.7 %collective-permute-start.13 = (f32[3,1,16,32,1]{3,2,4,1,0:T(8,128)S(1)}, f32[3,1,16,32,1]{3,2,4,1,0:T(8,128)S(1)}, u32[]{:S(2)}, u32[]{:S(2)}) collective-permute-start(f32[3,1,16,32,1]{3,2,4,1,0:T(8,128)S(1)} %copy.90), channel_id=1, source_target_pairs={{1,0},{2,1},{3,2},{4,3},{5,4},{6,5},{7,6},{0,7},{9,8},{10,9},{11,1... | collective-permute-start | bytes 18440 | tf_op jit(solution)/shard_map/ppermute | solution.py:22
  91.0 31.5 %collective-permute-start.17 = (f32[3,1,16,32,128]{4,3,2,1,0:T(8,128)}, f32[3,1,16,32,128]{4,3,2,1,0:T(8,128)S(1)}, u32[]{:S(2)}, u32[]{:S(2)}) collective-permute-start(f32[3,1,16,32,128]{4,3,2,1,0:T(8,128)} %collective-permute-done.16), channel_id=1, source_target_pairs={{0,128},{8,136},{16,144},{24,152},{32,160},{40,168},{48,176},{56,1... | collective-permute-start | bytes 2359304 | tf_op jit(solution)/shard_map/ppermute | solution.py:32
  93.3 5.6 %copy-start.6 = (f32[3,1,16,32,1]{3,2,4,1,0:T(8,128)}, f32[3,1,16,32,1]{3,2,4,1,0:T(8,128)S(1)}, u32[]{:S(2)}) copy-start(f32[3,1,16,32,1]{3,2,4,1,0:T(8,128)S(1)} %collective-permute-done.14) | copy-start | bytes 18436
  93.3 30.4 %collective-permute-start.12 = (f32[6,1,16,1,128]{4,2,3,1,0:T(8,128)}, f32[6,1,16,1,128]{4,2,3,1,0:T(8,128)S(1)}, u32[]{:S(2)}, u32[]{:S(2)}) collective-permute-start(f32[6,1,16,1,128]{4,2,3,1,0:T(8,128)} %bitcast.37), channel_id=1, source_target_pairs={{0,8},{8,16},{16,24},{1,9},{9,17},{17,25},{2,10},{10,18},{18,26},{... | collective-permute-start | bytes 147464 | tf_op jit(solution)/shard_map/ppermute | solution.py:20
  98.8 0.6 copy-start.8
  99.5 26.1 %collective-permute-start.11 = (f32[6,1,16,1,128]{4,2,3,1,0:T(8,128)}, f32[6,1,16,1,128]{4,2,3,1,0:T(8,128)}, u32[]{:S(2)}, u32[]{:S(2)}) collective-permute-start(f32[6,1,16,1,128]{4,2,3,1,0:T(8,128)} %bitcast.36), channel_id=1, source_target_pairs={{8,0},{16,8},{24,16},{9,1},{17,9},{25,17},{10,2},{18,10},{26,18},{... | collective-permute-start | bytes 147464 | tf_op jit(solution)/shard_map/ppermute | solution.py:22
  129.9 2.4 collective-permute-start.24
  132.3 20.6 %collective-permute-start.25 = (f32[3,1,16,32,128]{4,3,2,1,0:T(8,128)S(1)}, f32[3,1,16,32,128]{4,3,2,1,0:T(8,128)}, u32[]{:S(2)}, u32[]{:S(2)}) collective-permute-start(f32[3,1,16,32,128]{4,3,2,1,0:T(8,128)S(1)} %collective-permute-done.24), channel_id=1, source_target_pairs={{0,16},{8,24},{16,0},{24,8},{32,48},{40,56},{48,32},{56,40},{64,80... | collective-permute-start | bytes 2359304 | tf_op jit(solution)/shard_map/ppermute | solution.py:32
  133.2 57.2 %collective-permute-start.19 = (f32[3,1,16,32,128]{4,3,2,1,0:T(8,128)S(1)}, f32[3,1,16,32,128]{4,3,2,1,0:T(8,128)}, u32[]{:S(2)}, u32[]{:S(2)}) collective-permute-start(f32[3,1,16,32,128]{4,3,2,1,0:T(8,128)S(1)} %fusion.28), channel_id=1, source_target_pairs={{0,32},{32,64},{64,96},{96,128},{128,160},{160,192},{192,224},{224... | collective-permute-start | bytes 2359304 | tf_op jit(solution)/shard_map/ppermute | solution.py:20
  133.2 57.2 %collective-permute-start.18 = (f32[3,1,16,32,128]{4,3,2,1,0:T(8,128)S(1)}, f32[3,1,16,32,128]{4,3,2,1,0:T(8,128)}, u32[]{:S(2)}, u32[]{:S(2)}) collective-permute-start(f32[3,1,16,32,128]{4,3,2,1,0:T(8,128)S(1)} %fusion.28), channel_id=1, source_target_pairs={{32,0},{64,32},{96,64},{128,96},{160,128},{192,160},{224,192},{0,2... | collective-permute-start | bytes 2359304 | tf_op jit(solution)/shard_map/ppermute | solution.py:22
  152.8 35.6 %collective-permute-start.26 = (f32[3,1,16,32,128]{4,3,2,1,0:T(8,128)}, f32[3,1,16,32,128]{4,3,2,1,0:T(8,128)}, u32[]{:S(2)}, u32[]{:S(2)}) collective-permute-start(f32[3,1,16,32,128]{4,3,2,1,0:T(8,128)} %collective-permute-done.25), channel_id=1, source_target_pairs={{0,128},{8,136},{16,144},{24,152},{32,160},{40,168},{48,176},{56,1... | collective-permute-start | bytes 2359304 | tf_op jit(solution)/shard_map/ppermute | solution.py:32
  155.2 7.3 %collective-permute-start.23 = (f32[3,1,16,32,1]{3,2,4,1,0:T(8,128)S(1)}, f32[3,1,16,32,1]{3,2,4,1,0:T(8,128)S(1)}, u32[]{:S(2)}, u32[]{:S(2)}) collective-permute-start(f32[3,1,16,32,1]{3,2,4,1,0:T(8,128)S(1)} %copy.100), channel_id=1, source_target_pairs={{0,1},{1,2},{2,3},{3,4},{4,5},{5,6},{6,7},{7,0},{8,9},{9,10},{10,1... | collective-permute-start | bytes 18440 | tf_op jit(solution)/shard_map/ppermute | solution.py:20
  156.9 10.3 %collective-permute-start.22 = (f32[3,1,16,32,1]{3,2,4,1,0:T(8,128)S(1)}, f32[3,1,16,32,1]{3,2,4,1,0:T(8,128)S(1)}, u32[]{:S(2)}, u32[]{:S(2)}) collective-permute-start(f32[3,1,16,32,1]{3,2,4,1,0:T(8,128)S(1)} %copy.98), channel_id=1, source_target_pairs={{1,0},{2,1},{3,2},{4,3},{5,4},{6,5},{7,6},{0,7},{9,8},{10,9},{11,1... | collective-permute-start | bytes 18440 | tf_op jit(solution)/shard_map/ppermute | solution.py:22
  162.5 24.5 %collective-permute-start.20 = (f32[3,1,16,1,128]{4,2,3,1,0:T(8,128)S(1)}, f32[3,1,16,1,128]{4,2,3,1,0:T(8,128)S(1)}, u32[]{:S(2)}, u32[]{:S(2)}) collective-permute-start(f32[3,1,16,1,128]{4,2,3,1,0:T(8,128)S(1)} %bitcast.77), channel_id=1, source_target_pairs={{8,0},{16,8},{24,16},{9,1},{17,9},{25,17},{10,2},{18,10},{26,18},{... | collective-permute-start | bytes 73736 | tf_op jit(solution)/shard_map/ppermute | solution.py:22
  167.2 19.8 %collective-permute-start.21 = (f32[3,1,16,1,128]{4,2,3,1,0:T(8,128)S(1)}, f32[3,1,16,1,128]{4,2,3,1,0:T(8,128)S(1)}, u32[]{:S(2)}, u32[]{:S(2)}) collective-permute-start(f32[3,1,16,1,128]{4,2,3,1,0:T(8,128)S(1)} %bitcast.75), channel_id=1, source_target_pairs={{0,8},{8,16},{16,24},{1,9},{9,17},{17,25},{2,10},{10,18},{18,26},{... | collective-permute-start | bytes 73736 | tf_op jit(solution)/shard_map/ppermute | solution.py:20
  190.4 7.6 %copy-start.3 = (f32[3,1,15,32,128]{4,3,2,1,0:T(8,128)S(1)}, f32[3,1,15,32,128]{4,3,2,1,0:T(8,128)}, u32[]{:S(2)}) copy-start(f32[3,1,15,32,128]{4,3,2,1,0:T(8,128)} %get-tuple-element.29) | copy-start | bytes 2211844
  194.9 57.8 %copy-start.1 = (f32[3,1,16,32,128]{4,3,2,1,0:T(8,128)}, f32[3,1,16,32,128]{4,3,2,1,0:T(8,128)S(1)}, u32[]{:S(2)}) copy-start(f32[3,1,16,32,128]{4,3,2,1,0:T(8,128)S(1)} %get-tuple-element.10) | copy-start | bytes 2359300
  194.9 3.8 %copy-start.2 = (f32[3,1,15,32,128]{4,3,2,1,0:T(8,128)S(1)}, f32[3,1,15,32,128]{4,3,2,1,0:T(8,128)}, u32[]{:S(2)}) copy-start(f32[3,1,15,32,128]{4,3,2,1,0:T(8,128)} %get-tuple-element.30) | copy-start | bytes 2211844
  194.9 2.4 collective-permute-start.33
  197.3 20.8 %collective-permute-start.34 = (f32[3,1,16,32,128]{4,3,2,1,0:T(8,128)}, f32[3,1,16,32,128]{4,3,2,1,0:T(8,128)}, u32[]{:S(2)}, u32[]{:S(2)}) collective-permute-start(f32[3,1,16,32,128]{4,3,2,1,0:T(8,128)} %collective-permute-done.33), channel_id=1, source_target_pairs={{0,16},{8,24},{16,0},{24,8},{32,48},{40,56},{48,32},{56,40},{64,80... | collective-permute-start | bytes 2359304 | tf_op jit(solution)/shard_map/ppermute | solution.py:32
  199.4 53.2 %collective-permute-start.28 = (f32[3,1,16,32,128]{4,3,2,1,0:T(8,128)S(1)}, f32[3,1,16,32,128]{4,3,2,1,0:T(8,128)}, u32[]{:S(2)}, u32[]{:S(2)}) collective-permute-start(f32[3,1,16,32,128]{4,3,2,1,0:T(8,128)S(1)} %get-tuple-element.10), channel_id=1, source_target_pairs={{0,32},{32,64},{64,96},{96,128},{128,160},{160,192},{192,224},{224... | collective-permute-start | bytes 2359304 | tf_op jit(solution)/shard_map/ppermute | solution.py:20
  199.4 53.2 %collective-permute-start.27 = (f32[3,1,16,32,128]{4,3,2,1,0:T(8,128)S(1)}, f32[3,1,16,32,128]{4,3,2,1,0:T(8,128)}, u32[]{:S(2)}, u32[]{:S(2)}) collective-permute-start(f32[3,1,16,32,128]{4,3,2,1,0:T(8,128)S(1)} %get-tuple-element.10), channel_id=1, source_target_pairs={{32,0},{64,32},{96,64},{128,96},{160,128},{192,160},{224,192},{0,2... | collective-permute-start | bytes 2359304 | tf_op jit(solution)/shard_map/ppermute | solution.py:22
  203.3 15.4 %copy-start.11 = (f32[32]{0:T(128)S(1)}, f32[32]{0:T(128)}, u32[]{:S(2)}) copy-start(f32[32]{0:T(128)} %param.5) | copy-start | bytes 388
  204.0 16.9 %collective-permute-start.32 = (f32[3,1,16,32,1]{3,2,4,1,0:T(8,128)S(1)}, f32[3,1,16,32,1]{3,2,4,1,0:T(8,128)S(1)}, u32[]{:S(2)}, u32[]{:S(2)}) collective-permute-start(f32[3,1,16,32,1]{3,2,4,1,0:T(8,128)S(1)} %copy.108), channel_id=1, source_target_pairs={{0,1},{1,2},{2,3},{3,4},{4,5},{5,6},{6,7},{7,0},{8,9},{9,10},{10,1... | collective-permute-start | bytes 18440 | tf_op jit(solution)/shard_map/ppermute | solution.py:20
  205.7 20.5 %collective-permute-start.31 = (f32[3,1,16,32,1]{3,2,4,1,0:T(8,128)S(1)}, f32[3,1,16,32,1]{3,2,4,1,0:T(8,128)S(1)}, u32[]{:S(2)}, u32[]{:S(2)}) collective-permute-start(f32[3,1,16,32,1]{3,2,4,1,0:T(8,128)S(1)} %copy.106), channel_id=1, source_target_pairs={{1,0},{2,1},{3,2},{4,3},{5,4},{6,5},{7,6},{0,7},{9,8},{10,9},{11,1... | collective-permute-start | bytes 18440 | tf_op jit(solution)/shard_map/ppermute | solution.py:22
  218.1 31.9 %collective-permute-start.35 = (f32[3,1,16,32,128]{4,3,2,1,0:T(8,128)}, f32[3,1,16,32,128]{4,3,2,1,0:T(8,128)}, u32[]{:S(2)}, u32[]{:S(2)}) collective-permute-start(f32[3,1,16,32,128]{4,3,2,1,0:T(8,128)} %collective-permute-done.34), channel_id=1, source_target_pairs={{0,128},{8,136},{16,144},{24,152},{32,160},{40,168},{48,176},{56,1... | collective-permute-start | bytes 2359304 | tf_op jit(solution)/shard_map/ppermute | solution.py:32
  220.9 7.8 %copy-start.7 = (f32[3,1,16,32,1]{3,2,4,1,0:T(8,128)}, f32[3,1,16,32,1]{3,2,4,1,0:T(8,128)S(1)}, u32[]{:S(2)}) copy-start(f32[3,1,16,32,1]{3,2,4,1,0:T(8,128)S(1)} %collective-permute-done.32) | copy-start | bytes 18436
  220.9 31.0 %collective-permute-start.30 = (f32[6,1,16,1,128]{4,2,3,1,0:T(8,128)}, f32[6,1,16,1,128]{4,2,3,1,0:T(8,128)S(1)}, u32[]{:S(2)}, u32[]{:S(2)}) collective-permute-start(f32[6,1,16,1,128]{4,2,3,1,0:T(8,128)} %bitcast.39), channel_id=1, source_target_pairs={{0,8},{8,16},{16,24},{1,9},{9,17},{17,25},{2,10},{10,18},{18,26},{... | collective-permute-start | bytes 147464 | tf_op jit(solution)/shard_map/ppermute | solution.py:20
  226.2 0.6 copy-start.9
  226.8 25.8 %collective-permute-start.29 = (f32[6,1,16,1,128]{4,2,3,1,0:T(8,128)}, f32[6,1,16,1,128]{4,2,3,1,0:T(8,128)}, u32[]{:S(2)}, u32[]{:S(2)}) collective-permute-start(f32[6,1,16,1,128]{4,2,3,1,0:T(8,128)} %bitcast.38), channel_id=1, source_target_pairs={{8,0},{16,8},{24,16},{9,1},{17,9},{25,17},{10,2},{18,10},{26,18},{... | collective-permute-start | bytes 147464 | tf_op jit(solution)/shard_map/ppermute | solution.py:22
where the time goes:
time: 258 us
  waiting for transfers between devices  129 us (50%)
  starting transfers between devices  75.4 us (29%)
  local copies, waits for them, and re-layouts  26.5 us (10%)
  other arithmetic  25.5 us (10%)
    ppermute x12, waiting for transfers between devices, partner_2(): return lax.ppermute(value, axis, pairs)  83.6 us
    ppermute x12, waiting for transfers between devices, with_halo(): lax.ppermute(head, axis, [((i + 1) % count, i) for i in range(ends)])  43.9 us
    ppermute x12, starting transfers between devices, with_halo(): lax.ppermute(head, axis, [((i + 1) % count, i) for i in range(ends)])  41.8 us
    ppermute x12, starting transfers between devices, with_halo(): lax.ppermute(tail, axis, [(i, (i + 1) % count) for i in range(ends)])  25.8 us
    sub x2, other arithmetic, local(): present_state - step_rate * (local_part + 0.5 * (residual_now - mirror_re...  9.16 us
    reduce_sum x2, other arithmetic, descent_part(): jnp.sum(residual_now * slopes[component], axis=0)  8.98 us
    ppermute x12, starting transfers between devices, partner_2(): return lax.ppermute(value, axis, pairs)  7.81 us
    rev x4, local copies, waits for them, and re-layouts, reflect(): partner = partner[:, :, :, ::-1, :]  6.08 us
  transfers between devices with their start and end apart: 36, of which 15 were waited for; matrix products, arithmetic and copies ran while one was open for 13% of the time, Pallas kernels for 0%

commit v1 on v0

v1 whole, which is shorter than its diff:
```python
import jax
import jax.numpy as jnp
from jax import lax
from jax.experimental import pallas as pl
from jax.experimental.pallas import tpu as pltpu
from jax.sharding import PartitionSpec as P

STEP = 0.05
SIGN = (1.0, -1.0, 1.0)
MESH = pl.DeviceIdType.MESH
OFFSETS = [(dx, dy) for dx in range(4) for dy in range(4) if (dx, dy) != (0, 0)]
ROW0 = 8


def roll(v, shift, axis=1):
    return pltpu.roll(v, shift % 128 if isinstance(shift, int) else shift, axis)


def device_of(x, y, cls, z):
    xh, xl = x // 2, lax.rem(x, 2)
    return (xl * 4 + y, xh * 2 + (cls + xh - 2 * cls * xh), z)


def position():
    tm, wall, z = lax.axis_index("tm"), lax.axis_index("wall"), lax.axis_index("span")
    xl, y, xh, core = tm // 4, lax.rem(tm, 4), wall // 2, lax.rem(wall, 2)
    return xh * 2 + xl, y, core + xh - 2 * core * xh, z


def path_of(x, y):
    odd = lax.rem(y, 2)
    return 4 * y + x + odd * (3 - 2 * x)


def chip_at(p):
    y, a = p // 4, lax.rem(p, 4)
    odd = lax.rem(y, 2)
    return a + odd * (3 - 2 * a), y


def group_of(p, z):
    return p + lax.rem(z, 2) * (15 - 2 * p)


def slot_of(x, y):
    xh, xl = x // 2, lax.rem(x, 2)
    return xh, lax.rem(4 * xl + y + 4 * xh, 8)


def along_path(p, z, way):
    there = p + way * (1 - 2 * lax.rem(z, 2))
    over = (there + 16) // 16 - 1
    over = over * over
    x, y = chip_at(there * (1 - over) + p * over)
    return x, y, lax.rem(z + way * over + 8, 8)


def swap_groups(ins):
    lane = lax.broadcasted_iota(jnp.int32, (8, 128), 1)
    turned = [roll(v, 8 * i) for i, v in enumerate(ins)]
    mixed = [turned[-d % 16] for d in range(16)]
    for bit in range(4):
        mask = (lane & (8 << bit)) != 0
        mixed = [jnp.where(mask, mixed[(d - (1 << bit)) % 16], mixed[d]) for d in range(16)]
    return [roll(v, -8 * d) for d, v in enumerate(mixed)]


def frame_rows(v, xh):
    row = lax.broadcasted_iota(jnp.int32, (8, 128), 0)
    return jnp.take_along_axis(v, row + xh * (7 - 2 * row), axis=0, mode="promise_in_bounds")


def frame_sign(c, xh):
    xf = xh.astype(jnp.float32)
    return 1.0 - 2.0 * xf if SIGN[c] < 0 else None


def pack(src, dst, xh):
    def one(step, _):
        t = step
        to = t + xh * (3 - 2 * t)
        for c in range(3):
            sign = frame_sign(c, xh)
            ins = [src[c, i, pl.ds(pl.multiple_of(8 * t, 8), 8), :] for i in range(16)]
            for d, v in enumerate(swap_groups(ins)):
                v = frame_rows(v, xh)
                v = v if sign is None else v * sign
                dst[d, c, pl.ds(pl.multiple_of(8 * to, 8), 8), :] = v
        return 0

    lax.fori_loop(0, 4, one, 0)


def unpack(src, dst, xh):
    def one(step, _):
        t = step
        to = t + xh * (3 - 2 * t)
        for c in range(3):
            sign = frame_sign(c, xh)
            ins = [src[d, c, pl.ds(pl.multiple_of(8 * to, 8), 8), :] for d in range(16)]
            for i, v in enumerate(swap_groups(ins)):
                v = frame_rows(v, xh)
                v = v if sign is None else v * sign
                dst[c, i, pl.ds(pl.multiple_of(8 * t, 8), 8), :] = v
        return 0

    lax.fori_loop(0, 4, one, 0)


def pack_cells(field, left, right):
    cell = lax.broadcasted_iota(jnp.int32, (8, 128), 1) & 7

    def one(step, _):
        f, c = step // 3, lax.rem(step, 3)
        for t in range(4):
            lo = hi = None
            for n in range(8):
                v = field[f, n, c, ROW0 + 8 * t : ROW0 + 8 * t + 8, :]
                a, b = roll(v, n), roll(v, n - 7)
                lo = a if n == 0 else jnp.where(cell == n, a, lo)
                hi = b if n == 0 else jnp.where(cell == n, b, hi)
            left[f, c, 8 * t : 8 * t + 8, :] = lo
            right[f, c, 8 * t : 8 * t + 8, :] = hi
        return 0

    lax.fori_loop(0, 6, one, 0)


def pack_rows(field, edge, cls):
    def one(step, _):
        f, n = step // 8, lax.rem(step, 8)
        for c in range(3):
            first = field[f, n, c, ROW0 : ROW0 + 1, :]
            last = field[f, n, c, ROW0 + 31 : ROW0 + 32, :]
            edge[f, n, c : c + 1, :] = jnp.where(cls == 1, first, last)
        return 0

    lax.fori_loop(0, 16, one, 0)


def fill_rows(field, edge, cls):
    def one(step, _):
        f, n = step // 8, lax.rem(step, 8)
        for c in range(3):
            got = edge[f, n, c : c + 1, :]
            fold = SIGN[c] * field[1 - f, lax.rem(n + 4, 8), c, ROW0 + 31 : ROW0 + 32, :]
            field[f, n, c, ROW0 - 1 : ROW0, :] = jnp.where(cls == 1, got, 0.0)
            field[f, n, c, ROW0 + 32 : ROW0 + 33, :] = jnp.where(cls == 1, fold, got)
        return 0

    lax.fori_loop(0, 16, one, 0)


def shifts(field, left, right, f, n, c, t, cell):
    r0 = ROW0 + 8 * t
    v = field[f, n, c, r0 : r0 + 8, :]
    edge_hi = right[f, c, 8 * t : 8 * t + 8, :]
    edge_lo = left[f, c, 8 * t : 8 * t + 8, :]
    plane = (roll(v, -8), roll(v, 8))
    row = (field[f, n, c, r0 + 1 : r0 + 9, :], field[f, n, c, r0 - 1 : r0 + 7, :])
    span = (
        jnp.where(cell == 7, roll(edge_hi, 7 - n), roll(v, -1)),
        jnp.where(cell == 0, roll(edge_lo, lax.rem(128 - n, 128)), roll(v, 1)),
    )
    return v, plane, row, span


def residual_stage(field, left, right, nu, force, slopes, out):
    cell = lax.broadcasted_iota(jnp.int32, (8, 128), 1) & 7

    def one(step, _):
        f, n = step // 8, lax.rem(step, 8)
        ahead, behind = lax.rem(n + 1, 8), lax.rem(n + 7, 8)
        for t in range(4):
            r0 = ROW0 + 8 * t
            rows = slice(r0, r0 + 8)
            centre, slope, laps = [], [], []
            for c in range(3):
                v, plane, row, span = shifts(field, left, right, f, n, c, t, cell)
                d = [0.5 * (a - b) for a, b in (plane, row, span)]
                for axis in range(3):
                    slopes[f, n, axis, c, 8 * t : 8 * t + 8, :] = d[axis]
                lap = (plane[0] + plane[1]) + (row[0] + row[1]) + (span[0] + span[1]) - 6.0 * v
                centre.append(v)
                slope.append(d)
                laps.append(lap)
            mu = nu[f, rows, :]
            for c in range(3):
                s = slope[c]
                advect = centre[0] * s[0] + centre[1] * s[1] + centre[2] * s[2]
                drift = field[f, ahead, c, rows, :] - field[f, behind, c, rows, :]
                pull = centre[c] - field[1 - f, n, c, rows, :]
                value = 0.5 * (drift + pull) + advect - mu * laps[c]
                if force is not None:
                    value = value - force[f, n, c, 8 * t : 8 * t + 8, :]
                out[f, n, c, rows, :] = value
        return 0

    lax.fori_loop(0, 16, one, 0)


def subtract_stage(out, force):
    def one(step, _):
        f, n = step // 8, lax.rem(step, 8)
        for c in range(3):
            out[f, n, c, ROW0 : ROW0 + 32, :] = out[f, n, c, ROW0 : ROW0 + 32, :] - force[f, n, c]
        return 0

    lax.fori_loop(0, 16, one, 0)


def descent_stage(field, left, right, res, res_left, res_right, nu, slopes, out):
    cell = lax.broadcasted_iota(jnp.int32, (8, 128), 1) & 7

    def one(step, _):
        f, n = step // 8, lax.rem(step, 8)
        ahead, behind = lax.rem(n + 1, 8), lax.rem(n + 7, 8)
        for t in range(4):
            r0 = ROW0 + 8 * t
            rows = slice(r0, r0 + 8)
            mu, mu_up, mu_down = nu[f, rows, :], nu[f, r0 + 1 : r0 + 9, :], nu[f, r0 - 1 : r0 + 7, :]
            u0 = field[f, n, 0, rows, :]
            u2 = field[f, n, 2, rows, :]
            up0, um0 = roll(u0, -8), roll(u0, 8)
            up1, um1 = field[f, n, 1, r0 + 1 : r0 + 9, :], field[f, n, 1, r0 - 1 : r0 + 7, :]
            edge_hi = right[f, 2, 8 * t : 8 * t + 8, :]
            edge_lo = left[f, 2, 8 * t : 8 * t + 8, :]
            up2 = jnp.where(cell == 7, roll(edge_hi, 7 - n), roll(u2, -1))
            um2 = jnp.where(cell == 0, roll(edge_lo, lax.rem(128 - n, 128)), roll(u2, 1))
            every = [shifts(res, res_left, res_right, f, n, c, t, cell) for c in range(3)]
            for c in range(3):
                r, plane, row, span = every[c]
                transport = None
                for e in range(3):
                    term = every[e][0] * slopes[f, n, c, e, 8 * t : 8 * t + 8, :]
                    transport = term if transport is None else transport + term
                second = (up0 * plane[0] - um0 * plane[1]) + (up1 * row[0] - um1 * row[1])
                second = second + (up2 * span[0] - um2 * span[1])
                diffused = mu * ((plane[0] + plane[1]) + (span[0] + span[1]) - 6.0 * r)
                diffused = diffused + (mu_up * row[0] + mu_down * row[1])
                drift = res[f, behind, c, rows, :] - res[f, ahead, c, rows, :]
                pull = r - res[1 - f, n, c, rows, :]
                descent = 0.5 * (drift + pull - second) + transport - diffused
                out[f, n, c, rows, :] = field[f, n, c, rows, :] - STEP * descent
        return 0

    lax.fori_loop(0, 16, one, 0)


def kernel(
    u_hbm, f_hbm, nu_in, out_r, out_u,
    raw_u, raw_f, pack_u, pack_f, field_a, field_b, force, res, slopes, nu,
    cells_out, cells_in, rows_out, rows_in,
    load_sem, self_sem, u_send, u_recv, f_send, f_recv, r_send, r_recv, o_send, o_recv,
    halo_send, halo_recv, nu_send, nu_recv,
):
    x, y, cls, z = position()
    xh = x // 2
    p = path_of(x, y)
    group = group_of(p, z)
    my_f, my_n = slot_of(x, y)
    rows = pl.ds(ROW0, 32)

    load_u = pltpu.make_async_copy(u_hbm, raw_u, load_sem.at[0])
    load_u.start()
    load_f = pltpu.make_async_copy(f_hbm, raw_f, load_sem.at[1])
    load_f.start()

    barrier = pltpu.get_barrier_semaphore()
    peers = [(lax.rem(x + dx, 4), lax.rem(y + dy, 4)) for dx, dy in OFFSETS]
    for px, py in peers:
        pl.semaphore_signal(barrier, inc=1, device_id=device_of(px, py, cls, z), device_id_type=MESH)
    for there in (
        device_of(x, y, 1 - cls, z),
        device_of(x, y, cls, lax.rem(z + 1, 8)),
        device_of(x, y, cls, lax.rem(z + 7, 8)),
    ):
        pl.semaphore_signal(barrier, inc=1, device_id=there, device_id_type=MESH)

    row_id = lax.broadcasted_iota(jnp.int32, (8, 128), 0)
    for t in range(4):
        tile = jnp.zeros((8, 128), jnp.float32)
        for s in range(8):
            r = 8 * t + s
            tile = jnp.where(row_id == s, nu_in[r + xh * (31 - 2 * r)], tile)
        nu[xh, ROW0 + 8 * t : ROW0 + 8 * t + 8, :] = tile

    load_u.wait()
    pack(raw_u, pack_u, xh)
    pl.semaphore_wait(barrier, len(OFFSETS) + 3)

    def remote(src, dst, send, recv, there):
        return pltpu.make_async_remote_copy(
            src_ref=src, dst_ref=dst, send_sem=send, recv_sem=recv, device_id=there, device_id_type=MESH
        )

    pending = []
    u_in = []
    for j, (px, py) in enumerate(peers):
        copy = remote(
            pack_u.at[group_of(path_of(px, py), z)], field_a.at[my_f, my_n, :, rows],
            u_send.at[j], u_recv.at[j], device_of(px, py, cls, z),
        )
        copy.start()
        u_in.append(copy)
    own_u = pltpu.make_async_copy(pack_u.at[group], field_a.at[my_f, my_n, :, rows], self_sem.at[0])
    own_u.start()
    nu_copy = remote(nu.at[xh, rows], nu.at[xh, rows], nu_send, nu_recv, device_of(3 - x, y, cls, z))
    nu_copy.start()
    pending += u_in

    load_f.wait()
    pack(raw_f, pack_f, xh)
    f_in = []

    def send_force(c):
        for j, (px, py) in enumerate(peers):
            copy = remote(
                pack_f.at[group_of(path_of(px, py), z), c], force.at[my_f, my_n, c],
                f_send.at[c, j], f_recv.at[c, j], device_of(px, py, cls, z),
            )
            copy.start()
            f_in.append(copy)

    own_f = pltpu.make_async_copy(pack_f.at[group], force.at[my_f, my_n], self_sem.at[1])
    own_f.start()
    send_force(0)
    send_force(1)

    nx, ny, nz = along_path(p, z, 1)
    bx, by, bz = along_path(p, z, -1)
    ahead_dev, behind_dev = device_of(nx, ny, cls, nz), device_of(bx, by, cls, bz)
    other_core = device_of(x, y, 1 - cls, z)

    def send_halos(k, values):
        pack_cells(values, cells_out.at[k, 0], cells_out.at[k, 1])
        sends = [
            remote(cells_out.at[k, 0], cells_in.at[k, 1], halo_send.at[k, 0], halo_recv.at[k, 0], behind_dev),
            remote(cells_out.at[k, 1], cells_in.at[k, 0], halo_send.at[k, 1], halo_recv.at[k, 1], ahead_dev),
        ]
        for copy in sends:
            copy.start()
        pack_rows(values, rows_out.at[k], cls)
        if k == 0:
            for f in range(2):
                edge = jnp.where(cls == 1, nu[f, ROW0 : ROW0 + 1, :], nu[f, ROW0 + 31 : ROW0 + 32, :])
                rows_out[k, f, 0, 3:4, :] = edge
        sends.append(
            remote(rows_out.at[k], rows_in.at[k], halo_send.at[k, 2], halo_recv.at[k, 2], other_core)
        )
        sends[-1].start()
        pending.extend(sends)
        return sends

    def take_halos(k, values, sends):
        sends[2].wait_recv()
        fill_rows(values, rows_in.at[k], cls)
        if k == 0:
            for f in range(2):
                got = rows_in[k, f, 0, 3:4, :]
                fold = nu[1 - f, ROW0 + 31 : ROW0 + 32, :]
                nu[f, ROW0 - 1 : ROW0, :] = jnp.where(cls == 1, got, 0.0)
                nu[f, ROW0 + 32 : ROW0 + 33, :] = jnp.where(cls == 1, fold, got)
        sends[0].wait_recv()
        sends[1].wait_recv()

    nu_copy.wait()
    own_u.wait()
    for copy in u_in:
        copy.wait_recv()

    sends = send_halos(0, field_a)
    send_force(2)
    take_halos(0, field_a, sends)
    residual_stage(field_a, cells_in.at[0, 0], cells_in.at[0, 1], nu, None, slopes, res)
    own_f.wait()
    for copy in f_in:
        copy.wait_recv()
    pending += f_in
    subtract_stage(res, force)

    sends = send_halos(1, res)
    take_halos(1, res, sends)
    descent_stage(
        field_a, cells_in.at[0, 0], cells_in.at[0, 1], res, cells_in.at[1, 0], cells_in.at[1, 1],
        nu, slopes, field_b,
    )
    sends = send_halos(2, field_b)
    take_halos(2, field_b, sends)
    residual_stage(field_b, cells_in.at[2, 0], cells_in.at[2, 1], nu, force, slopes, res)
    sends = send_halos(3, res)

    def send_back(values, dst, send, recv):
        copies = []
        for j, (px, py) in enumerate(peers):
            f, n = slot_of(px, py)
            copy = remote(
                values.at[f, n, :, rows], dst.at[group], send.at[j], recv.at[j], device_of(px, py, cls, z)
            )
            copy.start()
            copies.append(copy)
        return copies

    r_out = send_back(res, out_r, r_send, r_recv)
    own_r = pltpu.make_async_copy(res.at[my_f, my_n, :, rows], out_r.at[group], self_sem.at[2])
    own_r.start()
    take_halos(3, res, sends)
    descent_stage(
        field_b, cells_in.at[2, 0], cells_in.at[2, 1], res, cells_in.at[3, 0], cells_in.at[3, 1],
        nu, slopes, field_a,
    )
    o_out = send_back(field_a, out_u, o_send, o_recv)
    own_o = pltpu.make_async_copy(field_a.at[my_f, my_n, :, rows], out_u.at[group], self_sem.at[3])
    own_o.start()
    own_r.wait()
    own_o.wait()
    for copy in pending:
        copy.wait_send()
    for copy in r_out + o_out:
        copy.wait()


def finish(r_in, u_in, u_out, r_out):
    x, _, _, _ = position()
    unpack(u_in, u_out, x // 2)
    unpack(r_in, r_out, x // 2)


def local(starting_speed_vector, driving_source, viscosity):
    block = starting_speed_vector.shape
    flat = (3, 16, 32, 128)
    f32 = jnp.float32
    packed = jax.ShapeDtypeStruct((16, 3, 32, 128), f32)
    dma = pltpu.SemaphoreType.DMA
    padded = pltpu.VMEM((2, 8, 3, 48, 128), f32)
    got_r, got_u = pl.pallas_call(
        kernel,
        out_shape=(packed, packed),
        in_specs=[
            pl.BlockSpec(memory_space=pl.ANY),
            pl.BlockSpec(memory_space=pl.ANY),
            pl.BlockSpec(memory_space=pltpu.SMEM),
        ],
        out_specs=(pl.BlockSpec(memory_space=pl.ANY),) * 2,
        scratch_shapes=[
            pltpu.VMEM(flat, f32),
            pltpu.VMEM(flat, f32),
            pltpu.VMEM((16, 3, 32, 128), f32),
            pltpu.VMEM((16, 3, 32, 128), f32),
            padded,
            padded,
            pltpu.VMEM((2, 8, 3, 32, 128), f32),
            padded,
            pltpu.VMEM((2, 8, 3, 3, 32, 128), f32),
            pltpu.VMEM((2, 48, 128), f32),
            pltpu.VMEM((4, 2, 2, 3, 32, 128), f32),
            pltpu.VMEM((4, 2, 2, 3, 32, 128), f32),
            pltpu.VMEM((4, 2, 8, 8, 128), f32),
            pltpu.VMEM((4, 2, 8, 8, 128), f32),
            dma((2,)), dma((4,)),
            dma((15,)), dma((15,)), dma((3, 15)), dma((3, 15)),
            dma((15,)), dma((15,)), dma((15,)), dma((15,)),
            dma((4, 3)), dma((4, 3)), dma(()), dma(()),
        ],
        compiler_params=pltpu.CompilerParams(
            collective_id=0, has_side_effects=True, vmem_limit_bytes=48 * 1024 * 1024
        ),
        name="descend",
    )(starting_speed_vector.reshape(flat), driving_source.reshape(flat), viscosity)
    orbit, residual = pl.pallas_call(
        finish,
        out_shape=(jax.ShapeDtypeStruct(flat, f32), jax.ShapeDtypeStruct(flat, f32)),
        in_specs=[pl.BlockSpec(memory_space=pltpu.VMEM)] * 2,
        out_specs=(pl.BlockSpec(memory_space=pltpu.VMEM),) * 2,
        name="finish",
    )(got_r, got_u)
    return orbit.reshape(block), residual.reshape(block)


def solution(mesh):
    spec = P(None, "tm", None, "wall", "span")
    return jax.shard_map(
        local, mesh=mesh, in_specs=(spec, spec, P("wall")), out_specs=(spec, spec), check_vma=False
    )
```

time: 258 us -> 83.1 us (0.32)
  waiting for transfers between devices: 129 us -> 0 us
  Pallas kernels: 0 us -> 77.2 us
  starting transfers between devices: 75.4 us -> 0 us
  other arithmetic: 25.5 us -> 0 us
  local copies, waits for them, and re-layouts: 26.5 us -> 4.69 us
    ppermute x36 -> x0, waiting for transfers between devices: 129 us -> none  [the longest x12 83.6 us: partner_2(): return lax.ppermute(value, axis, pairs)]
    pallas_call x0 -> x2, Pallas kernels: none -> 77.2 us  [the longest x1 73.2 us: local(): pl.pallas_call(kernel, out_shape=(packed, packed), in_specs=[pl.BlockSpec...]
    ppermute x36 -> x0, starting transfers between devices: 75.4 us -> none  [the longest x12 41.8 us: with_halo(): lax.ppermute(head, axis, [((i + 1) % count, i) for i in range(ends)])]
    slice x20 -> x0, local copies, waits for them, and re-layouts: 10 us -> none  [the longest x8 5.32 us: along_flow(): return (jnp.roll(values, -1, 2), jnp.roll(values, 1, 2))]
    sub x2 -> x0, other arithmetic: 9.16 us -> none  [local(): present_state - step_rate * (local_part + 0.5 * (residual_now - mirror_re...]
    reduce_sum x2 -> x0, other arithmetic: 8.98 us -> none  [descent_part(): jnp.sum(residual_now * slopes[component], axis=0)]
    ppermute x8 -> x0, local copies, waits for them, and re-layouts: 8.5 us -> none  [the longest x4 4.69 us: with_halo(): lax.ppermute(tail, axis, [(i, (i + 1) % count) for i in range(ends)])]
    rev x4 -> x0, local copies, waits for them, and re-layouts: 6.08 us -> none  [reflect(): partner = partner[:, :, :, ::-1, :]]
  transfers between devices with their start and end apart: 36 -> 0, of which waited for: 15 -> 0; matrix products, arithmetic and copies ran while one was open for 13% -> 0% of each run, Pallas kernels for 0% -> 0%
where the time goes in v1:
time: 83.1 us; the launch traced here: 82.6 us
  Pallas kernels  77.2 us (93%)
  local copies, waits for them, and re-layouts  4.69 us (6%)
    pallas_call x1, Pallas kernels, local(): pl.pallas_call(kernel, out_shape=(packed, packed), in_specs=[pl.BlockSpec...  73.2 us
    unnamed x10, local copies, waits for them, and re-layouts  4.69 us
    pallas_call x1, Pallas kernels, local(): pl.pallas_call(finish, out_shape=(jax.ShapeDtypeStruct(flat, f32), jax.Sh...  3.97 us

profile of v1, /device:TPU:1, one launch (start us, length us, event | category | flops | bytes accessed | tf_op | source)
XLA Modules:
  0.0 82.6 jit_solution(17700596971805782672)
XLA Ops:
  0.6 0.0 copy-start.4
  0.6 0.6 copy-done.4
  1.3 0.0 copy-start
  1.3 1.1 %copy-done = f32[3,1,16,32,128]{4,3,2,1,0:T(8,128)S(1)} copy-done((f32[3,1,16,32,128]{4,3,2,1,0:T(8,128)S(1)}, f32[3,1,16,32,128]{4,3,2,1,0:T(8,128)}, u32[]{:S(2)}) %copy-start) | copy-done | bytes 786456
  2.4 0.0 copy-start.1
  2.4 1.1 %copy-done.1 = f32[3,1,16,32,128]{4,3,2,1,0:T(8,128)S(1)} copy-done((f32[3,1,16,32,128]{4,3,2,1,0:T(8,128)S(1)}, f32[3,1,16,32,128]{4,3,2,1,0:T(8,128)}, u32[]{:S(2)}) %copy-start.1) | copy-done | bytes 786456
  3.6 73.2 %descend.1 = (f32[16,3,32,128]{3,2,1,0:T(8,128)S(1)}, f32[16,3,32,128]{3,2,1,0:T(8,128)S(1)}) custom-call(f32[3,16,32,128]{3,2,1,0:T(8,128)S(1)} %bitcast.8, f32[3,16,32,128]{3,2,1,0:T(8,128)S(1)} %bitcast.9, f32[32]{0:T(128)S(1)} %copy-done.4), custom_call_target="tpu_custom_call" | custom-call | tf_op jit(solution)/shard_map/descend/pallas_call | solution.py:436
  76.8 0.0 copy-start.2
  76.8 0.9 %copy-done.2 = f32[16,3,32,128]{3,2,1,0:T(8,128)} copy-done((f32[16,3,32,128]{3,2,1,0:T(8,128)}, f32[16,3,32,128]{3,2,1,0:T(8,128)S(1)}, u32[]{:S(2)}) %copy-start.2) | copy-done | bytes 786456
  77.7 0.0 copy-start.3
  77.7 0.9 %copy-done.3 = f32[16,3,32,128]{3,2,1,0:T(8,128)} copy-done((f32[16,3,32,128]{3,2,1,0:T(8,128)}, f32[16,3,32,128]{3,2,1,0:T(8,128)S(1)}, u32[]{:S(2)}) %copy-start.3) | copy-done | bytes 786456
  78.6 4.0 %finish.1 = (f32[3,16,32,128]{3,2,1,0:T(8,128)}, f32[3,16,32,128]{3,2,1,0:T(8,128)}) custom-call(f32[16,3,32,128]{3,2,1,0:T(8,128)} %copy-done.2, f32[16,3,32,128]{3,2,1,0:T(8,128)} %copy-done.3), custom_call_target="tpu_custom_call" | custom-call | tf_op jit(solution)/shard_map/finish/pallas_call | solution.py:470
Async XLA Ops:
  0.6 0.7 copy-start.4
  1.3 1.1 %copy-start = (f32[3,1,16,32,128]{4,3,2,1,0:T(8,128)S(1)}, f32[3,1,16,32,128]{4,3,2,1,0:T(8,128)}, u32[]{:S(2)}) copy-start(f32[3,1,16,32,128]{4,3,2,1,0:T(8,128)} %param.3) | copy-start | bytes 2359300
  2.4 1.1 %copy-start.1 = (f32[3,1,16,32,128]{4,3,2,1,0:T(8,128)S(1)}, f32[3,1,16,32,128]{4,3,2,1,0:T(8,128)}, u32[]{:S(2)}) copy-start(f32[3,1,16,32,128]{4,3,2,1,0:T(8,128)} %param.4) | copy-start | bytes 2359300
  76.8 0.9 %copy-start.2 = (f32[16,3,32,128]{3,2,1,0:T(8,128)}, f32[16,3,32,128]{3,2,1,0:T(8,128)S(1)}, u32[]{:S(2)}) copy-start(f32[16,3,32,128]{3,2,1,0:T(8,128)S(1)} %get-tuple-element.6.r_in) | copy-start | bytes 2359300
  77.7 0.9 %copy-start.3 = (f32[16,3,32,128]{3,2,1,0:T(8,128)}, f32[16,3,32,128]{3,2,1,0:T(8,128)S(1)}, u32[]{:S(2)}) copy-start(f32[16,3,32,128]{3,2,1,0:T(8,128)S(1)} %get-tuple-element.7.u_in) | copy-start | bytes 2359300

commit v2 on v1

v2 whole, which is shorter than its diff:
```python
import jax
import jax.numpy as jnp
from jax import lax
from jax.experimental import pallas as pl
from jax.experimental.pallas import tpu as pltpu
from jax.sharding import PartitionSpec as P

STEP = 0.05
SIGN = (1.0, -1.0, 1.0)
MESH = pl.DeviceIdType.MESH
OFFSETS = [(dx, dy) for dx in range(4) for dy in range(4) if (dx, dy) != (0, 0)]
ROW0 = 8


def roll(v, shift, axis=1):
    return pltpu.roll(v, shift % 128 if isinstance(shift, int) else shift, axis)


def device_of(x, y, cls, z):
    xh, xl = x // 2, lax.rem(x, 2)
    return (xl * 4 + y, xh * 2 + (cls + xh - 2 * cls * xh), z)


def position():
    tm, wall, z = lax.axis_index("tm"), lax.axis_index("wall"), lax.axis_index("span")
    xl, y, xh, core = tm // 4, lax.rem(tm, 4), wall // 2, lax.rem(wall, 2)
    return xh * 2 + xl, y, core + xh - 2 * core * xh, z


def path_of(x, y):
    odd = lax.rem(y, 2)
    return 4 * y + x + odd * (3 - 2 * x)


def chip_at(p):
    y, a = p // 4, lax.rem(p, 4)
    odd = lax.rem(y, 2)
    return a + odd * (3 - 2 * a), y


def group_of(p, z):
    return p + lax.rem(z, 2) * (15 - 2 * p)


def slot_of(x, y):
    xh, xl = x // 2, lax.rem(x, 2)
    return xh, lax.rem(4 * xl + y + 4 * xh, 8)


def along_path(p, z, way):
    there = p + way * (1 - 2 * lax.rem(z, 2))
    over = (there + 16) // 16 - 1
    over = over * over
    x, y = chip_at(there * (1 - over) + p * over)
    return x, y, lax.rem(z + way * over + 8, 8)


def swap_groups(ins, before=0, after=0):
    lane = lax.broadcasted_iota(jnp.int32, (8, 128), 1)
    turned = [roll(v, lax.rem(8 * i + before + 128, 128)) for i, v in enumerate(ins)]
    mixed = [turned[-d % 16] for d in range(16)]
    for bit in range(4):
        mask = (lane & (8 << bit)) != 0
        mixed = [jnp.where(mask, mixed[(d - (1 << bit)) % 16], mixed[d]) for d in range(16)]
    return [roll(v, lax.rem(128 - 8 * d + after, 128)) for d, v in enumerate(mixed)]


def frame_rows(v, xh):
    row = lax.broadcasted_iota(jnp.int32, (8, 128), 0)
    return jnp.take_along_axis(v, row + xh * (7 - 2 * row), axis=0, mode="promise_in_bounds")


def frame_sign(v, c, xh):
    return v * (1.0 - 2.0 * xh.astype(jnp.float32)) if SIGN[c] < 0 else v


def tile(t):
    return pl.ds(pl.multiple_of(8 * t, 8), 8)


def pack(src, dst, xh, n):
    def one(t, _):
        to = tile(t + xh * (3 - 2 * t))
        for c in range(3):
            ins = [src[c, i, tile(t), :] for i in range(16)]
            for d, v in enumerate(swap_groups(ins, 0, n)):
                dst[d, c, to, :] = frame_sign(frame_rows(v, xh), c, xh)
        return 0

    lax.fori_loop(0, 4, one, 0)


def unpack_rows(src, dst, xh, n, t):
    to = tile(t + xh * (3 - 2 * t))
    for c in range(3):
        ins = [src[d, c, to, :] for d in range(16)]
        for i, v in enumerate(swap_groups(ins, -n, 0)):
            dst[c, i, tile(t), :] = frame_sign(frame_rows(v, xh), c, xh)


def unpack(src, dst, xh, n):
    def one(t, _):
        unpack_rows(src, dst, xh, n, t)
        return 0

    lax.fori_loop(0, 4, one, 0)


def residues():
    lane = lax.broadcasted_iota(jnp.int32, (8, 128), 1) & 7
    return [lane == q for q in range(8)]


class Edges:
    def __init__(self):
        self.first = self.last = None

    def add(self, masks, n, v):
        self.first = v if n == 0 else jnp.where(masks[n], v, self.first)
        self.last = v if n == 0 else jnp.where(masks[(n + 7) % 8], v, self.last)

    def store(self, out, f, c, t):
        out[f, 0, c, tile(t), :] = roll(self.first, 7)
        out[f, 1, c, tile(t), :] = roll(self.last, -7)


def pack_cells(field, out, f):
    masks = residues()

    def one(t, _):
        for c in range(3):
            edges = Edges()
            for n in range(8):
                edges.add(masks, n, field[f, n, c, tile(t + 1), :])
            edges.store(out, f, c, t)
        return 0

    lax.fori_loop(0, 4, one, 0)


def pack_rows(field, edge, final, cls):
    for f in range(2):
        for n in range(8):
            for c in range(3):
                first = field[f, n, c, ROW0 : ROW0 + 1, :]
                last = field[f, n, c, ROW0 + 31 : ROW0 + 32, :]
                edge[f, n, c : c + 1, :] = jnp.where(cls == 1, first, last)
                final[f, n, c : c + 1, :] = last


def fill_rows(field, edge, final, cls):
    row = lax.broadcasted_iota(jnp.int32, (8, 128), 0)
    sign = jnp.where(row == 1, SIGN[1], 1.0)
    for f in range(2):
        for n in range(8):
            got = edge[f, n]
            fold = sign * roll(final[1 - f, (n + 4) % 8], -4 if n < 4 else 4)
            low = jnp.where(cls == 1, got, 0.0)
            high = jnp.where(cls == 1, fold, got)
            for c in range(3):
                field[f, n, c, ROW0 - 1 : ROW0, :] = low[c : c + 1, :]
                field[f, n, c, ROW0 + 32 : ROW0 + 33, :] = high[c : c + 1, :]


def rotate_all(field, turned, wrap):
    def one(f, _):
        for c in range(3):
            for t in range(4):
                rows, out = slice(ROW0 + 8 * t, ROW0 + 8 * t + 8), slice(8 * t, 8 * t + 8)
                for n in range(8):
                    v = field[f, n, c, rows, :]
                    for kind, shift in enumerate((-8, 8, -1, 1)):
                        turned[kind, f, n, c, out, :] = roll(v, shift)
                    if n == 0:
                        wrap[0, f, c, out, :] = roll(v, 7)
                    if n == 7:
                        wrap[1, f, c, out, :] = roll(v, -7)
        return 0

    lax.fori_loop(0, 2, one, 0)


def times(turned, wrap, f, n, c, rows):
    ahead = wrap[0, f, c, rows, :] if n == 7 else turned[2, f, n + 1, c, rows, :]
    behind = wrap[1, f, c, rows, :] if n == 0 else turned[3, f, n - 1, c, rows, :]
    return ahead, behind


def residual_before(field, nu, turned, wrap, slopes, out):
    def one(step, _):
        f, t = step // 4, lax.rem(step, 4)
        rows = tile(t)
        mu = nu[f, tile(t + 1), :]
        for n in range(8):
            view = [field.at[f, n, c, pl.ds(pl.multiple_of(8 * t, 8), 24)] for c in range(3)]
            u0, u1 = view[0][8:16, :], view[1][8:16, :]
            for c in range(3):
                v, up, down = view[c][8:16, :], view[c][9:17, :], view[c][7:15, :]
                right, left = turned[0, f, n, c, rows, :], turned[1, f, n, c, rows, :]
                ahead, behind = times(turned, wrap, f, n, c, rows)
                along = 0.5 * (right - left)
                across = 0.5 * (up - down)
                slopes[f, n, 0, c, rows, :] = along
                slopes[f, n, 1, c, rows, :] = across
                lap = (right + left) + (up + down) - 6.0 * v
                pull = (ahead - behind) + (v - field[1 - f, n, c, tile(t + 1), :])
                out[f, n, c, rows, :] = 0.5 * pull + (u0 * along + u1 * across) - mu * lap
        return 0

    lax.fori_loop(0, 8, one, 0)


def residual_after(field, nu, turned, halo, force, partial, slopes, sides, out, cells, f):
    masks = residues()

    def one(t, _):
        rows, inner = tile(t), tile(t + 1)
        mu = nu[f, inner, :]
        for c in range(3):
            edges = Edges()
            high, low = halo[f, 0, c, rows, :], halo[f, 1, c, rows, :]
            for n in range(8):
                ahead = jnp.where(masks[(n + 7) % 8], high, turned[2, f, n, c, rows, :])
                behind = jnp.where(masks[n], low, turned[3, f, n, c, rows, :])
                slope = 0.5 * (ahead - behind)
                slopes[f, n, 2, c, rows, :] = slope
                if c == 2:
                    sides[0, f, n, rows, :] = ahead
                    sides[1, f, n, rows, :] = behind
                value = partial[f, n, c, rows, :] - force[f, n, c, rows, :]
                value = value + field[f, n, 2, inner, :] * slope - mu * (ahead + behind)
                out[f, n, c, inner, :] = value
                edges.add(masks, n, value)
            edges.store(cells, f, c, t)
        return 0

    lax.fori_loop(0, 4, one, 0)


def descent_before(field, res, nu, turned_u, turned, wrap, slopes, out):
    def one(step, _):
        f, t = step // 4, lax.rem(step, 4)
        rows, inner = tile(t), tile(t + 1)
        mus = nu.at[f, pl.ds(pl.multiple_of(8 * t, 8), 24)]
        mu, mu_up, mu_down = mus[8:16, :], mus[9:17, :], mus[7:15, :]
        for n in range(8):
            u1 = field.at[f, n, 1, pl.ds(pl.multiple_of(8 * t, 8), 24)]
            right0, left0 = 0.5 * turned_u[0, f, n, 0, rows, :], 0.5 * turned_u[1, f, n, 0, rows, :]
            up1, down1 = 0.5 * u1[9:17, :] + mu_up, 0.5 * u1[7:15, :] - mu_down
            centre = [res[f, n, e, inner, :] for e in range(3)]
            for c in range(3):
                r, view = centre[c], res.at[f, n, c, pl.ds(pl.multiple_of(8 * t, 8), 24)]
                right, left = turned[0, f, n, c, rows, :], turned[1, f, n, c, rows, :]
                ahead, behind = times(turned, wrap, f, n, c, rows)
                transport = centre[0] * slopes[f, n, c, 0, rows, :]
                transport = transport + centre[1] * slopes[f, n, c, 1, rows, :]
                transport = transport + centre[2] * slopes[f, n, c, 2, rows, :]
                flux = (right0 * right - left0 * left) + (up1 * view[9:17, :] - down1 * view[7:15, :])
                flux = flux + mu * ((right + left) - 6.0 * r)
                pull = (behind - ahead) + (r - res[1 - f, n, c, inner, :])
                descent = 0.5 * pull + (transport - flux)
                out[f, n, c, rows, :] = field[f, n, c, inner, :] - STEP * descent
        return 0

    lax.fori_loop(0, 8, one, 0)


def descent_after(nu, turned, halo, partial, sides, out, cells, f):
    masks = residues()

    def one(t, _):
        rows, inner = tile(t), tile(t + 1)
        mu = STEP * nu[f, inner, :]
        for c in range(3):
            edges = Edges()
            high, low = halo[f, 0, c, rows, :], halo[f, 1, c, rows, :]
            for n in range(8):
                ahead = jnp.where(masks[(n + 7) % 8], high, turned[2, f, n, c, rows, :])
                behind = jnp.where(masks[n], low, turned[3, f, n, c, rows, :])
                flux = sides[0, f, n, rows, :] * ahead - sides[1, f, n, rows, :] * behind
                value = partial[f, n, c, rows, :] + (0.5 * STEP * flux + mu * (ahead + behind))
                out[f, n, c, inner, :] = value
                if cells is not None:
                    edges.add(masks, n, value)
            if cells is not None:
                edges.store(cells, f, c, t)
        return 0

    lax.fori_loop(0, 4, one, 0)


def kernel(
    u_hbm, f_hbm, nu_in, out_r, out_u,
    raw_u, raw_f, pack_u, pack_f, field_a, field_b, force, res, partial, slopes, sides, nu,
    turned_u, turned_r, wrap, got_r, cells_out, cells_in, rows_out, rows_in, final,
    load_sem, self_sem, u_send, u_recv, f_send, f_recv, r_send, r_recv, o_send, o_recv,
    halo_send, halo_recv, nu_send, nu_recv,
):
    x, y, cls, z = position()
    xh = x // 2
    p = path_of(x, y)
    group = group_of(p, z)
    my_f, my_n = slot_of(x, y)
    rows = pl.ds(ROW0, 32)

    load_u = pltpu.make_async_copy(u_hbm, raw_u, load_sem.at[0])
    load_u.start()
    load_f = pltpu.make_async_copy(f_hbm, raw_f, load_sem.at[1])
    load_f.start()

    barrier = pltpu.get_barrier_semaphore()
    peers = [(lax.rem(x + dx, 4), lax.rem(y + dy, 4)) for dx, dy in OFFSETS]
    nx, ny, nz = along_path(p, z, 1)
    bx, by, bz = along_path(p, z, -1)
    ahead_dev, behind_dev = device_of(nx, ny, cls, nz), device_of(bx, by, cls, bz)
    other_core = device_of(x, y, 1 - cls, z)
    for px, py in peers:
        pl.semaphore_signal(barrier, inc=1, device_id=device_of(px, py, cls, z), device_id_type=MESH)
    for there in (
        other_core,
        device_of(x, y, cls, lax.rem(z + 1, 8)),
        device_of(x, y, cls, lax.rem(z + 7, 8)),
    ):
        pl.semaphore_signal(barrier, inc=1, device_id=there, device_id_type=MESH)

    row_id = lax.broadcasted_iota(jnp.int32, (8, 128), 0)
    for t in range(4):
        column = jnp.zeros((8, 128), jnp.float32)
        for s in range(8):
            r = 8 * t + s
            column = jnp.where(row_id == s, nu_in[r + xh * (31 - 2 * r)], column)
        nu[xh, ROW0 + 8 * t : ROW0 + 8 * t + 8, :] = column

    load_u.wait()
    pack(raw_u, pack_u, xh, my_n)
    pl.semaphore_wait(barrier, len(OFFSETS) + 3)

    def remote(src, dst, send, recv, there):
        return pltpu.make_async_remote_copy(
            src_ref=src, dst_ref=dst, send_sem=send, recv_sem=recv, device_id=there, device_id_type=MESH
        )

    pending = []
    u_in = []
    for j, (px, py) in enumerate(peers):
        copy = remote(
            pack_u.at[group_of(path_of(px, py), z)], field_a.at[my_f, my_n, :, rows],
            u_send.at[j], u_recv.at[j], device_of(px, py, cls, z),
        )
        copy.start()
        u_in.append(copy)
    own_u = pltpu.make_async_copy(pack_u.at[group], field_a.at[my_f, my_n, :, rows], self_sem.at[0])
    own_u.start()
    nu_copy = remote(nu.at[xh, rows], nu.at[xh, rows], nu_send, nu_recv, device_of(3 - x, y, cls, z))
    nu_copy.start()
    pending += u_in

    load_f.wait()
    pack(raw_f, pack_f, xh, my_n)
    f_in = []

    def send_force(c):
        for j, (px, py) in enumerate(peers):
            copy = remote(
                pack_f.at[group_of(path_of(px, py), z), c], force.at[my_f, my_n, c],
                f_send.at[c, j], f_recv.at[c, j], device_of(px, py, cls, z),
            )
            copy.start()
            f_in.append(copy)

    own_f = pltpu.make_async_copy(pack_f.at[group], force.at[my_f, my_n], self_sem.at[1])
    own_f.start()
    send_force(0)
    send_force(1)

    def send_cells(k, f):
        sends = [
            remote(
                cells_out.at[k, f, side], cells_in.at[k, f, side],
                halo_send.at[k, 2 * f + side], halo_recv.at[k, 2 * f + side], there,
            )
            for side, there in enumerate((behind_dev, ahead_dev))
        ]
        for copy in sends:
            copy.start()
        pending.extend(sends)
        return sends

    def send_rows(k, values):
        pack_rows(values, rows_out.at[k], final, cls)
        if k == 0:
            for f in range(2):
                edge = jnp.where(cls == 1, nu[f, ROW0 : ROW0 + 1, :], nu[f, ROW0 + 31 : ROW0 + 32, :])
                rows_out[k, f, 0, 3:4, :] = edge
        copy = remote(rows_out.at[k], rows_in.at[k], halo_send.at[k, 4], halo_recv.at[k, 4], other_core)
        copy.start()
        pending.append(copy)
        return copy

    def take_rows(k, values, copy):
        copy.wait_recv()
        fill_rows(values, rows_in.at[k], final, cls)
        if k == 0:
            for f in range(2):
                got = rows_in[k, f, 0, 3:4, :]
                fold = nu[1 - f, ROW0 + 31 : ROW0 + 32, :]
                nu[f, ROW0 - 1 : ROW0, :] = jnp.where(cls == 1, got, 0.0)
                nu[f, ROW0 + 32 : ROW0 + 33, :] = jnp.where(cls == 1, fold, got)

    def take_cells(sends):
        for copy in sends:
            copy.wait_recv()

    def residual_round(k, values, sends, last):
        edge = send_rows(k, values)
        rotate_all(values, turned_u, wrap)
        take_rows(k, values, edge)
        residual_before(values, nu, turned_u, wrap, slopes, partial)
        if not last:
            own_f.wait()
            for copy in f_in:
                copy.wait_recv()
        nexts = []
        for f in range(2):
            take_cells(sends[f])
            residual_after(
                values, nu, turned_u, cells_in.at[k], force, partial, slopes, sides, res,
                cells_out.at[k + 1], f,
            )
            nexts.append(send_cells(k + 1, f))
        return nexts

    def descent_round(k, values, sends, out, last):
        edge = send_rows(k, res)
        rotate_all(res, turned_r, wrap)
        take_rows(k, res, edge)
        descent_before(values, res, nu, turned_u, turned_r, wrap, slopes, partial)
        nexts = []
        for f in range(2):
            take_cells(sends[f])
            descent_after(
                nu, turned_r, cells_in.at[k], partial, sides, out,
                None if last else cells_out.at[k + 1], f,
            )
            if not last:
                nexts.append(send_cells(k + 1, f))
        return nexts

    def send_back(values, dst, send, recv):
        copies = []
        for j, (px, py) in enumerate(peers):
            f, n = slot_of(px, py)
            copy = remote(
                values.at[f, n, :, rows], dst.at[group], send.at[j], recv.at[j], device_of(px, py, cls, z)
            )
            copy.start()
            copies.append(copy)
        return copies

    nu_copy.wait()
    own_u.wait()
    take_cells(u_in)

    sends = []
    for f in range(2):
        pack_cells(field_a, cells_out.at[0], f)
        sends.append(send_cells(0, f))
    send_force(2)
    sends = residual_round(0, field_a, sends, False)
    pending += f_in
    sends = descent_round(1, field_a, sends, field_b, False)
    sends = residual_round(2, field_b, sends, True)

    r_out = send_back(res, got_r, r_send, r_recv)
    own_r = pltpu.make_async_copy(res.at[my_f, my_n, :, rows], got_r.at[group], self_sem.at[2])
    own_r.start()
    descent_round(3, field_b, sends, field_a, True)
    o_out = send_back(field_a, out_u, o_send, o_recv)
    own_o = pltpu.make_async_copy(field_a.at[my_f, my_n, :, rows], out_u.at[group], self_sem.at[3])
    own_o.start()

    own_r.wait()
    take_cells(r_out)
    unpack(got_r, raw_u, xh, my_n)
    store_r = pltpu.make_async_copy(raw_u, out_r, load_sem.at[0])
    store_r.start()
    for copy in pending + r_out:
        copy.wait_send()
    store_r.wait()
    own_o.wait()
    for copy in o_out:
        copy.wait()


def finish(u_hbm, r_hbm, u_out, r_out, packed, plain, passed, u_load, u_store, r_sem):
    x, y, _, _ = position()
    xh = x // 2
    _, n = slot_of(x, y)
    loads, stores = [], []
    for t in range(4):
        here, there = tile(t), tile(t + xh * (3 - 2 * t))
        loads.append(pltpu.make_async_copy(u_hbm.at[:, :, there], packed.at[:, :, there], u_load.at[t]))
        stores.append(pltpu.make_async_copy(plain.at[:, :, here], u_out.at[:, :, here], u_store.at[t]))
        loads[-1].start()
    through = pltpu.make_async_copy(r_hbm, passed, r_sem.at[0])
    through.start()
    for t in range(4):
        loads[t].wait()
        unpack_rows(packed, plain, xh, n, t)
        stores[t].start()
        if t == 0:
            through.wait()
            onward = pltpu.make_async_copy(passed, r_out, r_sem.at[1])
            onward.start()
    for copy in stores + [onward]:
        copy.wait()


def local(starting_speed_vector, driving_source, viscosity):
    block = starting_speed_vector.shape
    f32 = jnp.float32
    flat = (3, 16, 32, 128)
    plain, packed = pltpu.VMEM(flat, f32), pltpu.VMEM((16, 3, 32, 128), f32)
    slabs, padded = pltpu.VMEM((2, 8, 3, 32, 128), f32), pltpu.VMEM((2, 8, 3, 48, 128), f32)
    turned = pltpu.VMEM((4, 2, 8, 3, 32, 128), f32)
    cells = pltpu.VMEM((4, 2, 2, 3, 32, 128), f32)
    edge = pltpu.VMEM((4, 2, 8, 8, 128), f32)
    dma = pltpu.SemaphoreType.DMA
    anywhere = pl.BlockSpec(memory_space=pl.ANY)
    got_r, got_u = pl.pallas_call(
        kernel,
        out_shape=(jax.ShapeDtypeStruct(flat, f32), jax.ShapeDtypeStruct((16, 3, 32, 128), f32)),
        in_specs=[anywhere, anywhere, pl.BlockSpec(memory_space=pltpu.SMEM)],
        out_specs=(anywhere, anywhere),
        scratch_shapes=[
            plain, plain, packed, packed, padded, padded, slabs, padded, slabs,
            pltpu.VMEM((2, 8, 3, 3, 32, 128), f32),
            pltpu.VMEM((2, 2, 8, 32, 128), f32),
            pltpu.VMEM((2, 48, 128), f32),
            turned, turned,
            pltpu.VMEM((2, 2, 3, 32, 128), f32),
            packed, cells, cells, edge, edge,
            pltpu.VMEM((2, 8, 8, 128), f32),
            dma((2,)), dma((4,)),
            dma((15,)), dma((15,)), dma((3, 15)), dma((3, 15)),
            dma((15,)), dma((15,)), dma((15,)), dma((15,)),
            dma((4, 5)), dma((4, 5)), dma(()), dma(()),
        ],
        compiler_params=pltpu.CompilerParams(collective_id=0, has_side_effects=True),
        name="descend",
    )(starting_speed_vector.reshape(flat), driving_source.reshape(flat), viscosity)
    orbit, residual = pl.pallas_call(
        finish,
        out_shape=(jax.ShapeDtypeStruct(flat, f32), jax.ShapeDtypeStruct(flat, f32)),
        in_specs=[anywhere, anywhere],
        out_specs=(anywhere, anywhere),
        scratch_shapes=[packed, plain, plain, dma((4,)), dma((4,)), dma((2,))],
        name="finish",
    )(got_u, got_r)
    return orbit.reshape(block), residual.reshape(block)


def solution(mesh):
    spec = P(None, "tm", None, "wall", "span")
    return jax.shard_map(
        local, mesh=mesh, in_specs=(spec, spec, P("wall")), out_specs=(spec, spec), check_vma=False
    )
```

time: 83.1 us -> 69.5 us (0.84)
  Pallas kernels: 77.2 us -> 68.3 us
  local copies, waits for them, and re-layouts: 4.69 us -> 0 us
    pallas_call x1, Pallas kernels: 73.2 us -> 65.5 us  [local(): pl.pallas_call(kernel, out_shape=(jax.ShapeDtypeStruct(flat, f32), jax.Sh...]
    unnamed x10 -> x0, local copies, waits for them, and re-layouts: 4.69 us -> none
    pallas_call x1, Pallas kernels: 3.97 us -> 2.77 us  [local(): pl.pallas_call(finish, out_shape=(jax.ShapeDtypeStruct(flat, f32), jax.Sh...]
where the time goes in v2:
time: 69.5 us; the launch traced here: 68.9 us
  Pallas kernels  68.3 us (98%)
    pallas_call x1, Pallas kernels, local(): pl.pallas_call(kernel, out_shape=(jax.ShapeDtypeStruct(flat, f32), jax.Sh...  65.5 us
    pallas_call x1, Pallas kernels, local(): pl.pallas_call(finish, out_shape=(jax.ShapeDtypeStruct(flat, f32), jax.Sh...  2.77 us

profile of v2, /device:TPU:1, one launch (start us, length us, event | category | flops | bytes accessed | tf_op | source)
XLA Modules:
  0.0 68.9 jit_solution(2676088777374376484)
XLA Ops:
  0.6 65.5 %descend.1 = (f32[3,16,32,128]{3,2,1,0:T(8,128)}, f32[16,3,32,128]{3,2,1,0:T(8,128)}) custom-call(f32[3,16,32,128]{3,2,1,0:T(8,128)} %bitcast.8, f32[3,16,32,128]{3,2,1,0:T(8,128)} %bitcast.9, f32[32]{0:T(128)} %nu_in.1), custom_call_target="tpu_custom_call" | custom-call | tf_op jit(solution)/shard_map/descend/pallas_call | solution.py:530
  66.1 2.8 %finish.1 = (f32[3,16,32,128]{3,2,1,0:T(8,128)}, f32[3,16,32,128]{3,2,1,0:T(8,128)}) custom-call(f32[16,3,32,128]{3,2,1,0:T(8,128)} %get-tuple-element.6.u_hbm, f32[3,16,32,128]{3,2,1,0:T(8,128)} %get-tuple-element.7.r_hbm), custom_call_target="tpu_custom_call" | custom-call | tf_op jit(solution)/shard_map/finish/pallas_call | solution.py:552

commit v3 on v2

--- a/solution.py
+++ b/solution.py
@@ -8,7 +8,10 @@
 STEP = 0.05
 SIGN = (1.0, -1.0, 1.0)
 MESH = pl.DeviceIdType.MESH
-OFFSETS = [(dx, dy) for dx in range(4) for dy in range(4) if (dx, dy) != (0, 0)]
+OFFSETS = sorted(
+    ((dx, dy) for dx in range(4) for dy in range(4) if (dx, dy) != (0, 0)),
+    key=lambda o: -(min(o[0], 4 - o[0]) + min(o[1], 4 - o[1])),
+)
 ROW0 = 8
 
 
@@ -120,19 +123,20 @@
         self.last = v if n == 0 else jnp.where(masks[(n + 7) % 8], v, self.last)
 
     def store(self, out, f, c, t):
-        out[f, 0, c, tile(t), :] = roll(self.first, 7)
-        out[f, 1, c, tile(t), :] = roll(self.last, -7)
-
-
-def pack_cells(field, out, f):
+        out[0, f, c, tile(t), :] = roll(self.first, 7)
+        out[1, f, c, tile(t), :] = roll(self.last, -7)
+
+
+def pack_cells(field, out, h):
     masks = residues()
 
-    def one(t, _):
+    def one(step, _):
+        f, part = step // 2, lax.rem(step, 2)
         for c in range(3):
             edges = Edges()
             for n in range(8):
-                edges.add(masks, n, field[f, n, c, tile(t + 1), :])
-            edges.store(out, f, c, t)
+                edges.add(masks, n, field[f, n, c, tile(part + 2 * h + 1), :])
+            edges.store(out, f, c, part)
         return 0
 
     lax.fori_loop(0, 4, one, 0)
@@ -210,15 +214,17 @@
     lax.fori_loop(0, 8, one, 0)
 
 
-def residual_after(field, nu, turned, halo, force, partial, slopes, sides, out, cells, f):
+def residual_after(field, nu, turned, halo, force, partial, slopes, sides, out, cells, h):
     masks = residues()
 
-    def one(t, _):
+    def one(step, _):
+        f, part = step // 2, lax.rem(step, 2)
+        t = part + 2 * h
         rows, inner = tile(t), tile(t + 1)
         mu = nu[f, inner, :]
         for c in range(3):
             edges = Edges()
-            high, low = halo[f, 0, c, rows, :], halo[f, 1, c, rows, :]
+            high, low = halo[0, f, c, tile(part), :], halo[1, f, c, tile(part), :]
             for n in range(8):
                 ahead = jnp.where(masks[(n + 7) % 8], high, turned[2, f, n, c, rows, :])
                 behind = jnp.where(masks[n], low, turned[3, f, n, c, rows, :])
@@ -231,7 +237,7 @@
                 value = value + field[f, n, 2, inner, :] * slope - mu * (ahead + behind)
                 out[f, n, c, inner, :] = value
                 edges.add(masks, n, value)
-            edges.store(cells, f, c, t)
+            edges.store(cells, f, c, part)
         return 0
 
     lax.fori_loop(0, 4, one, 0)
@@ -265,15 +271,17 @@
     lax.fori_loop(0, 8, one, 0)
 
 
-def descent_after(nu, turned, halo, partial, sides, out, cells, f):
+def descent_after(nu, turned, halo, partial, sides, out, cells, h):
     masks = residues()
 
-    def one(t, _):
+    def one(step, _):
+        f, part = step // 2, lax.rem(step, 2)
+        t = part + 2 * h
         rows, inner = tile(t), tile(t + 1)
         mu = STEP * nu[f, inner, :]
         for c in range(3):
             edges = Edges()
-            high, low = halo[f, 0, c, rows, :], halo[f, 1, c, rows, :]
+            high, low = halo[0, f, c, tile(part), :], halo[1, f, c, tile(part), :]
             for n in range(8):
                 ahead = jnp.where(masks[(n + 7) % 8], high, turned[2, f, n, c, rows, :])
                 behind = jnp.where(masks[n], low, turned[3, f, n, c, rows, :])
@@ -283,7 +291,7 @@
                 if cells is not None:
                     edges.add(masks, n, value)
             if cells is not None:
-                edges.store(cells, f, c, t)
+                edges.store(cells, f, c, part)
         return 0
 
     lax.fori_loop(0, 4, one, 0)
@@ -359,11 +367,12 @@
     pack(raw_f, pack_f, xh, my_n)
     f_in = []
 
-    def send_force(c):
+    def send_force(h):
+        half = pl.ds(16 * h, 16)
         for j, (px, py) in enumerate(peers):
             copy = remote(
-                pack_f.at[group_of(path_of(px, py), z), c], force.at[my_f, my_n, c],
-                f_send.at[c, j], f_recv.at[c, j], device_of(px, py, cls, z),
+                pack_f.at[group_of(path_of(px, py), z), :, half], force.at[my_f, my_n, :, half],
+                f_send.at[h, j], f_recv.at[h, j], device_of(px, py, cls, z),
             )
             copy.start()
             f_in.append(copy)
@@ -371,13 +380,12 @@
     own_f = pltpu.make_async_copy(pack_f.at[group], force.at[my_f, my_n], self_sem.at[1])
     own_f.start()
     send_force(0)
-    send_force(1)
-
-    def send_cells(k, f):
+
+    def send_cells(k, h):
         sends = [
             remote(
-                cells_out.at[k, f, side], cells_in.at[k, f, side],
-                halo_send.at[k, 2 * f + side], halo_recv.at[k, 2 * f + side], there,
+                cells_out.at[k, h, side], cells_in.at[k, h, side],
+                halo_send.at[k, 2 * h + side], halo_recv.at[k, 2 * h + side], there,
             )
             for side, there in enumerate((behind_dev, ahead_dev))
         ]
@@ -418,16 +426,16 @@
         residual_before(values, nu, turned_u, wrap, slopes, partial)
         if not last:
             own_f.wait()
-            for copy in f_in:
-                copy.wait_recv()
         nexts = []
-        for f in range(2):
-            take_cells(sends[f])
+        for h in range(2):
+            take_cells(sends[h])
+            if not last:
+                take_cells(f_in[15 * h : 15 * h + 15])
             residual_after(
-                values, nu, turned_u, cells_in.at[k], force, partial, slopes, sides, res,
-                cells_out.at[k + 1], f,
+                values, nu, turned_u, cells_in.at[k, h], force, partial, slopes, sides, res,
+                cells_out.at[k + 1, h], h,
             )
-            nexts.append(send_cells(k + 1, f))
+            nexts.append(send_cells(k + 1, h))
         return nexts
 
     def descent_round(k, values, sends, out, last):
@@ -436,14 +444,14 @@
         take_rows(k, res, edge)
         descent_before(values, res, nu, turned_u, turned_r, wrap, slopes, partial)
         nexts = []
-        for f in range(2):
-            take_cells(sends[f])
+        for h in range(2):
+            take_cells(sends[h])
             descent_after(
-                nu, turned_r, cells_in.at[k], partial, sides, out,
-                None if last else cells_out.at[k + 1], f,
+                nu, turned_r, cells_in.at[k, h], partial, sides, out,
+                None if last else cells_out.at[k + 1, h], h,
             )
             if not last:
-                nexts.append(send_cells(k + 1, f))
+                nexts.append(send_cells(k + 1, h))
         return nexts
 
     def send_back(values, dst, send, recv):
@@ -462,10 +470,10 @@
     take_cells(u_in)
 
     sends = []
-    for f in range(2):
-        pack_cells(field_a, cells_out.at[0], f)
-        sends.append(send_cells(0, f))
-    send_force(2)
+    for h in range(2):
+        pack_cells(field_a, cells_out.at[0, h], h)
+        sends.append(send_cells(0, h))
+    send_force(1)
     sends = residual_round(0, field_a, sends, False)
     pending += f_in
     sends = descent_round(1, field_a, sends, field_b, False)
@@ -523,7 +531,7 @@
     plain, packed = pltpu.VMEM(flat, f32), pltpu.VMEM((16, 3, 32, 128), f32)
     slabs, padded = pltpu.VMEM((2, 8, 3, 32, 128), f32), pltpu.VMEM((2, 8, 3, 48, 128), f32)
     turned = pltpu.VMEM((4, 2, 8, 3, 32, 128), f32)
-    cells = pltpu.VMEM((4, 2, 2, 3, 32, 128), f32)
+    cells = pltpu.VMEM((4, 2, 2, 2, 3, 16, 128), f32)
     edge = pltpu.VMEM((4, 2, 8, 8, 128), f32)
     dma = pltpu.SemaphoreType.DMA
     anywhere = pl.BlockSpec(memory_space=pl.ANY)
@@ -542,7 +550,7 @@
             packed, cells, cells, edge, edge,
             pltpu.VMEM((2, 8, 8, 128), f32),
             dma((2,)), dma((4,)),
-            dma((15,)), dma((15,)), dma((3, 15)), dma((3, 15)),
+            dma((15,)), dma((15,)), dma((2, 15)), dma((2, 15)),
             dma((15,)), dma((15,)), dma((15,)), dma((15,)),
             dma((4, 5)), dma((4, 5)), dma(()), dma(()),
         ],

time: 69.5 us -> 65.7 us (0.945)
  Pallas kernels: 68.3 us -> 64.5 us
    pallas_call x1, Pallas kernels: 65.5 us -> 61.7 us  [local(): pl.pallas_call(kernel, out_shape=(jax.ShapeDtypeStruct(flat, f32), jax.Sh...]
where the time goes in v3:
time: 65.7 us; the launch traced here: 65.1 us
  Pallas kernels  64.5 us (98%)
    pallas_call x1, Pallas kernels, local(): pl.pallas_call(kernel, out_shape=(jax.ShapeDtypeStruct(flat, f32), jax.Sh...  61.7 us
    pallas_call x1, Pallas kernels, local(): pl.pallas_call(finish, out_shape=(jax.ShapeDtypeStruct(flat, f32), jax.Sh...  2.77 us

profile of v3, /device:TPU:1, one launch (start us, length us, event | category | flops | bytes accessed | tf_op | source)
XLA Modules:
  0.0 65.1 jit_solution(7722890388136895679)
XLA Ops:
  0.6 61.7 %descend.1 = (f32[3,16,32,128]{3,2,1,0:T(8,128)}, f32[16,3,32,128]{3,2,1,0:T(8,128)}) custom-call(f32[3,16,32,128]{3,2,1,0:T(8,128)} %bitcast.8, f32[3,16,32,128]{3,2,1,0:T(8,128)} %bitcast.9, f32[32]{0:T(128)} %nu_in.1), custom_call_target="tpu_custom_call" | custom-call | tf_op jit(solution)/shard_map/descend/pallas_call | solution.py:538
  62.3 2.8 %finish.1 = (f32[3,16,32,128]{3,2,1,0:T(8,128)}, f32[3,16,32,128]{3,2,1,0:T(8,128)}) custom-call(f32[16,3,32,128]{3,2,1,0:T(8,128)} %get-tuple-element.6.u_hbm, f32[3,16,32,128]{3,2,1,0:T(8,128)} %get-tuple-element.7.r_hbm), custom_call_target="tpu_custom_call" | custom-call | tf_op jit(solution)/shard_map/finish/pallas_call | solution.py:560

commit v4 on v3

--- a/solution.py
+++ b/solution.py
@@ -122,24 +122,23 @@
         self.first = v if n == 0 else jnp.where(masks[n], v, self.first)
         self.last = v if n == 0 else jnp.where(masks[(n + 7) % 8], v, self.last)
 
-    def store(self, out, f, c, t):
-        out[0, f, c, tile(t), :] = roll(self.first, 7)
-        out[1, f, c, tile(t), :] = roll(self.last, -7)
-
-
-def pack_cells(field, out, h):
+    def store(self, out, f, c):
+        out[0, f, c] = roll(self.first, 7)
+        out[1, f, c] = roll(self.last, -7)
+
+
+def pack_cells(field, out, t):
     masks = residues()
 
-    def one(step, _):
-        f, part = step // 2, lax.rem(step, 2)
+    def one(f, _):
         for c in range(3):
             edges = Edges()
             for n in range(8):
-                edges.add(masks, n, field[f, n, c, tile(part + 2 * h + 1), :])
-            edges.store(out, f, c, part)
-        return 0
-
-    lax.fori_loop(0, 4, one, 0)
+                edges.add(masks, n, field[f, n, c, ROW0 + 8 * t : ROW0 + 8 * t + 8, :])
+            edges.store(out, f, c)
+        return 0
+
+    lax.fori_loop(0, 2, one, 0)
 
 
 def pack_rows(field, edge, final, cls):
@@ -214,17 +213,16 @@
     lax.fori_loop(0, 8, one, 0)
 
 
-def residual_after(field, nu, turned, halo, force, partial, slopes, sides, out, cells, h):
+def residual_after(field, nu, turned, halo, force, partial, slopes, sides, out, cells, t):
     masks = residues()
 
-    def one(step, _):
-        f, part = step // 2, lax.rem(step, 2)
-        t = part + 2 * h
-        rows, inner = tile(t), tile(t + 1)
+    rows, inner = slice(8 * t, 8 * t + 8), slice(ROW0 + 8 * t, ROW0 + 8 * t + 8)
+
+    def one(f, _):
         mu = nu[f, inner, :]
         for c in range(3):
             edges = Edges()
-            high, low = halo[0, f, c, tile(part), :], halo[1, f, c, tile(part), :]
+            high, low = halo[0, f, c], halo[1, f, c]
             for n in range(8):
                 ahead = jnp.where(masks[(n + 7) % 8], high, turned[2, f, n, c, rows, :])
                 behind = jnp.where(masks[n], low, turned[3, f, n, c, rows, :])
@@ -237,10 +235,10 @@
                 value = value + field[f, n, 2, inner, :] * slope - mu * (ahead + behind)
                 out[f, n, c, inner, :] = value
                 edges.add(masks, n, value)
-            edges.store(cells, f, c, part)
-        return 0
-
-    lax.fori_loop(0, 4, one, 0)
+            edges.store(cells, f, c)
+        return 0
+
+    lax.fori_loop(0, 2, one, 0)
 
 
 def descent_before(field, res, nu, turned_u, turned, wrap, slopes, out):
@@ -271,17 +269,16 @@
     lax.fori_loop(0, 8, one, 0)
 
 
-def descent_after(nu, turned, halo, partial, sides, out, cells, h):
+def descent_after(nu, turned, halo, partial, sides, out, cells, t):
     masks = residues()
 
-    def one(step, _):
-        f, part = step // 2, lax.rem(step, 2)
-        t = part + 2 * h
-        rows, inner = tile(t), tile(t + 1)
+    rows, inner = slice(8 * t, 8 * t + 8), slice(ROW0 + 8 * t, ROW0 + 8 * t + 8)
+
+    def one(f, _):
         mu = STEP * nu[f, inner, :]
         for c in range(3):
             edges = Edges()
-            high, low = halo[0, f, c, tile(part), :], halo[1, f, c, tile(part), :]
+            high, low = halo[0, f, c], halo[1, f, c]
             for n in range(8):
                 ahead = jnp.where(masks[(n + 7) % 8], high, turned[2, f, n, c, rows, :])
                 behind = jnp.where(masks[n], low, turned[3, f, n, c, rows, :])
@@ -291,10 +288,10 @@
                 if cells is not None:
                     edges.add(masks, n, value)
             if cells is not None:
-                edges.store(cells, f, c, part)
-        return 0
-
-    lax.fori_loop(0, 4, one, 0)
+                edges.store(cells, f, c)
+        return 0
+
+    lax.fori_loop(0, 2, one, 0)
 
 
 def kernel(
@@ -400,7 +397,7 @@
             for f in range(2):
                 edge = jnp.where(cls == 1, nu[f, ROW0 : ROW0 + 1, :], nu[f, ROW0 + 31 : ROW0 + 32, :])
                 rows_out[k, f, 0, 3:4, :] = edge
-        copy = remote(rows_out.at[k], rows_in.at[k], halo_send.at[k, 4], halo_recv.at[k, 4], other_core)
+        copy = remote(rows_out.at[k], rows_in.at[k], halo_send.at[k, 8], halo_recv.at[k, 8], other_core)
         copy.start()
         pending.append(copy)
         return copy
@@ -427,10 +424,10 @@
         if not last:
             own_f.wait()
         nexts = []
-        for h in range(2):
+        for h in range(4):
             take_cells(sends[h])
-            if not last:
-                take_cells(f_in[15 * h : 15 * h + 15])
+            if not last and h % 2 == 0:
+                take_cells(f_in[15 * (h // 2) : 15 * (h // 2) + 15])
             residual_after(
                 values, nu, turned_u, cells_in.at[k, h], force, partial, slopes, sides, res,
                 cells_out.at[k + 1, h], h,
@@ -444,7 +441,7 @@
         take_rows(k, res, edge)
         descent_before(values, res, nu, turned_u, turned_r, wrap, slopes, partial)
         nexts = []
-        for h in range(2):
+        for h in range(4):
             take_cells(sends[h])
             descent_after(
                 nu, turned_r, cells_in.at[k, h], partial, sides, out,
@@ -470,7 +467,7 @@
     take_cells(u_in)
 
     sends = []
-    for h in range(2):
+    for h in range(4):
         pack_cells(field_a, cells_out.at[0, h], h)
         sends.append(send_cells(0, h))
     send_force(1)
@@ -531,7 +528,7 @@
     plain, packed = pltpu.VMEM(flat, f32), pltpu.VMEM((16, 3, 32, 128), f32)
     slabs, padded = pltpu.VMEM((2, 8, 3, 32, 128), f32), pltpu.VMEM((2, 8, 3, 48, 128), f32)
     turned = pltpu.VMEM((4, 2, 8, 3, 32, 128), f32)
-    cells = pltpu.VMEM((4, 2, 2, 2, 3, 16, 128), f32)
+    cells = pltpu.VMEM((4, 4, 2, 2, 3, 8, 128), f32)
     edge = pltpu.VMEM((4, 2, 8, 8, 128), f32)
     dma = pltpu.SemaphoreType.DMA
     anywhere = pl.BlockSpec(memory_space=pl.ANY)
@@ -552,7 +549,7 @@
             dma((2,)), dma((4,)),
             dma((15,)), dma((15,)), dma((2, 15)), dma((2, 15)),
             dma((15,)), dma((15,)), dma((15,)), dma((15,)),
-            dma((4, 5)), dma((4, 5)), dma(()), dma(()),
+            dma((4, 9)), dma((4, 9)), dma(()), dma(()),
         ],
         compiler_params=pltpu.CompilerParams(collective_id=0, has_side_effects=True),
         name="descend",

time: 65.7 us -> 65.1 us (level)
  no operation moved by 1% of the time
where the time goes in v4:
time: 65.1 us; the launch traced here: 64.6 us
  Pallas kernels  63.9 us (98%)
    pallas_call x1, Pallas kernels, local(): pl.pallas_call(kernel, out_shape=(jax.ShapeDtypeStruct(flat, f32), jax.Sh...  61.2 us
    pallas_call x1, Pallas kernels, local(): pl.pallas_call(finish, out_shape=(jax.ShapeDtypeStruct(flat, f32), jax.Sh...  2.77 us

profile of v4, /device:TPU:1, one launch (start us, length us, event | category | flops | bytes accessed | tf_op | source)
XLA Modules:
  0.0 64.6 jit_solution(13057441813434109279)
XLA Ops:
  0.6 61.2 %descend.1 = (f32[3,16,32,128]{3,2,1,0:T(8,128)}, f32[16,3,32,128]{3,2,1,0:T(8,128)}) custom-call(f32[3,16,32,128]{3,2,1,0:T(8,128)} %bitcast.8, f32[3,16,32,128]{3,2,1,0:T(8,128)} %bitcast.9, f32[32]{0:T(128)} %nu_in.1), custom_call_target="tpu_custom_call" | custom-call | tf_op jit(solution)/shard_map/descend/pallas_call | solution.py:535
  61.8 2.8 %finish.1 = (f32[3,16,32,128]{3,2,1,0:T(8,128)}, f32[3,16,32,128]{3,2,1,0:T(8,128)}) custom-call(f32[16,3,32,128]{3,2,1,0:T(8,128)} %get-tuple-element.6.u_hbm, f32[3,16,32,128]{3,2,1,0:T(8,128)} %get-tuple-element.7.r_hbm), custom_call_target="tpu_custom_call" | custom-call | tf_op jit(solution)/shard_map/finish/pallas_call | solution.py:557

commit v5 on v4

--- a/solution.py
+++ b/solution.py
@@ -138,7 +138,8 @@
             edges.store(out, f, c)
         return 0
 
-    lax.fori_loop(0, 2, one, 0)
+    one(0, 0)
+    one(1, 0)
 
 
 def pack_rows(field, edge, final, cls):
@@ -180,7 +181,8 @@
                         wrap[1, f, c, out, :] = roll(v, -7)
         return 0
 
-    lax.fori_loop(0, 2, one, 0)
+    one(0, 0)
+    one(1, 0)
 
 
 def times(turned, wrap, f, n, c, rows):
@@ -238,7 +240,8 @@
             edges.store(cells, f, c)
         return 0
 
-    lax.fori_loop(0, 2, one, 0)
+    one(0, 0)
+    one(1, 0)
 
 
 def descent_before(field, res, nu, turned_u, turned, wrap, slopes, out):
@@ -291,7 +294,8 @@
                 edges.store(cells, f, c)
         return 0
 
-    lax.fori_loop(0, 2, one, 0)
+    one(0, 0)
+    one(1, 0)
 
 
 def kernel(
@@ -507,8 +511,9 @@
         loads.append(pltpu.make_async_copy(u_hbm.at[:, :, there], packed.at[:, :, there], u_load.at[t]))
         stores.append(pltpu.make_async_copy(plain.at[:, :, here], u_out.at[:, :, here], u_store.at[t]))
         loads[-1].start()
-    through = pltpu.make_async_copy(r_hbm, passed, r_sem.at[0])
-    through.start()
+        if t == 0:
+            through = pltpu.make_async_copy(r_hbm, passed, r_sem.at[0])
+            through.start()
     for t in range(4):
         loads[t].wait()
         unpack_rows(packed, plain, xh, n, t)

time: 65.1 us -> 64.7 us (level)
  no operation moved by 1% of the time
where the time goes in v5:
time: 64.7 us; the launch traced here: 64.1 us
  Pallas kernels  63.5 us (98%)
    pallas_call x1, Pallas kernels, local(): pl.pallas_call(kernel, out_shape=(jax.ShapeDtypeStruct(flat, f32), jax.Sh...  60.7 us
    pallas_call x1, Pallas kernels, local(): pl.pallas_call(finish, out_shape=(jax.ShapeDtypeStruct(flat, f32), jax.Sh...  2.77 us

profile of v5, /device:TPU:1, one launch (start us, length us, event | category | flops | bytes accessed | tf_op | source)
XLA Modules:
  0.0 64.1 jit_solution(16356466231356797874)
XLA Ops:
  0.6 60.7 %descend.1 = (f32[3,16,32,128]{3,2,1,0:T(8,128)}, f32[16,3,32,128]{3,2,1,0:T(8,128)}) custom-call(f32[3,16,32,128]{3,2,1,0:T(8,128)} %bitcast.8, f32[3,16,32,128]{3,2,1,0:T(8,128)} %bitcast.9, f32[32]{0:T(128)} %nu_in.1), custom_call_target="tpu_custom_call" | custom-call | tf_op jit(solution)/shard_map/descend/pallas_call | solution.py:540
  61.4 2.8 %finish.1 = (f32[3,16,32,128]{3,2,1,0:T(8,128)}, f32[3,16,32,128]{3,2,1,0:T(8,128)}) custom-call(f32[16,3,32,128]{3,2,1,0:T(8,128)} %get-tuple-element.6.u_hbm, f32[3,16,32,128]{3,2,1,0:T(8,128)} %get-tuple-element.7.r_hbm), custom_call_target="tpu_custom_call" | custom-call | tf_op jit(solution)/shard_map/finish/pallas_call | solution.py:562
